TPU v7x, 32 devices: a whole 2x2x4 slice. The times are simulated.
32 devices in a mesh: clip: 2 (over x), seq: 16 (over z, y, core).
Axes of the slice: x: 2, y: 2, z: 4, core: 2. Of those that a mesh axis runs over, the one named last changes fastest.
Arguments:
- hidden: bfloat16 [2, 1792, 1536], P(None, ('clip', 'seq')), parts along dimension 1, may hold values from -6 to 6
- latent: float32 [1792, 100], P(('clip', 'seq')), parts along dimension 0, may hold values from -6 to 6
- lengths: int32 [2], P('clip'), parts along dimension 0, may hold values from 448 to 896
- step_index: int32 [1], replicated, may hold values from 0 to 31
- guidance: float32 [1], replicated, may hold values from 1.5 to 2.5
- modulation: float32 [5, 1536], replicated, may hold values from -2.5 to 2.5
- conv_kernel: float32 [31, 1536], replicated, may hold values from -1 to 1
- w_qkv: bfloat16 [1536, 3072], replicated, may hold values from -1 to 1
- w_out: bfloat16 [1024, 1536], replicated, may hold values from -0.1875 to 0.1875
- w_mel: bfloat16 [1536, 100], replicated, may hold values from -0.15625 to 0.15625
Outputs:
- velocity: float32 [1792, 100], P(('clip', 'seq')), parts along dimension 0
- estimate: float32 [1792, 100], P(('clip', 'seq')), parts along dimension 0
There are 2 independent parts, one for each index of `clip`. A program takes and returns all parts, laid end to end along the dimension named above; an argument that names none is the same for every part. Nothing has to cross between parts.
All inputs are finite; a program needn't handle non-finite values.
Results may differ from a plain program's by a relative error of at most 0.0061.
Values may be sent and summed in bfloat16 or wider, within the bound.
No kernel may reach another device: no remote copies, remote signals or barrier semaphores. Data moves between devices by JAX's collectives and lax.ppermute only.
A program may use at most 192 MiB of HBM per device.

v0:
```python
import functools

import jax
import jax.numpy as jnp
from jax import lax
from jax.experimental import pallas as pl
from jax.experimental.pallas import tpu as pltpu
from jax.sharding import PartitionSpec as P


HEADS = 16
HEAD_DIM = 64
KERNEL = 31
STEPS = 32
LANES = 128
HALO = 16


EPSILON = 1e-06
NEGATIVE = -1e30
CORE, CHIP, LENGTH = 0, 1, 2
VMEM = pltpu.VMEM
SMEM = pltpu.SMEM
MIB = 1 << 20


def vmem_spec():
    return pl.BlockSpec(memory_space=VMEM)


def smem_spec():
    return pl.BlockSpec(memory_space=SMEM)


def rotary_tables(positions):
    half_dim = HEAD_DIM // 2
    lane = jnp.arange(LANES, dtype=jnp.int32)
    inverse = 10000.0 ** (-(lane % half_dim).astype(jnp.float32) / half_dim)
    angles = positions.astype(jnp.float32)[:, None] * inverse[None, :]
    sign = jnp.where(lane % HEAD_DIM < half_dim, -1.0, 1.0)
    return jnp.cos(angles), jnp.sin(angles) * sign[None, :]


def hbm_spec():
    return pl.BlockSpec(memory_space=pltpu.HBM)


def tile_lanes(tile):
    return pl.ds(pl.multiple_of(tile * LANES, LANES), LANES)


def row_norm(load, store, tiles, mod_ref, row, total):
    width = tiles * LANES
    mean = jnp.sum(total, axis=-1, keepdims=True) * (1.0 / width)

    def square(tile, acc):
        centered = load(tile) - mean
        return acc + centered * centered

    squares = lax.fori_loop(0, tiles, square, jnp.zeros(total.shape, jnp.float32), unroll=6)
    variance = jnp.sum(squares, axis=-1, keepdims=True) * (1.0 / width)
    factor = lax.rsqrt(variance + EPSILON)

    def write(tile, carry):
        lanes = tile_lanes(tile)
        scale = 1.0 + mod_ref[row + 1 : row + 2, lanes]
        shift = mod_ref[row : row + 1, lanes]
        store(lanes, (load(tile) - mean) * factor * scale + shift)
        return carry

    lax.fori_loop(0, tiles, write, 0, unroll=6)


def run_copies(pairs, sems):
    copies = [
        pltpu.make_async_copy(source, target, sems.at[at])
        for at, (source, target) in enumerate(pairs)
    ]
    for copy in copies:
        copy.start()
    for copy in copies:
        copy.wait()


def edge_kernel(info_ref, hidden_hbm, near_ref, far_ref, sems):
    core = info_ref[CORE]
    edge = pl.ds(pl.multiple_of(core * (hidden_hbm.shape[1] - HALO), 8), HALO)
    run_copies(
        [(hidden_hbm.at[1 - core, edge], near_ref), (hidden_hbm.at[core, edge], far_ref)], sems
    )


def stage_kernel(info_ref, hidden_hbm, taps_hbm, mod_hbm, own_ref, taps_ref, mod_ref, sems):
    run_copies(
        [
            (hidden_hbm.at[info_ref[CORE]], own_ref),
            (taps_hbm, taps_ref),
            (mod_hbm, mod_ref),
        ],
        sems,
    )


def fetch_kernel(info_ref, residual_hbm, w_mel_hbm, residual_ref, w_mel_ref, sems):
    del info_ref
    run_copies([(residual_hbm, residual_ref), (w_mel_hbm, w_mel_ref)], sems)


def front_kernel(
    info_ref, own_ref, partner_ref, near_ref, far_ref, taps_ref, mod_ref, weight_hbm,
    residual_ref, normed_ref, weight_ref, padded, sems,
):
    rows, width = own_ref.shape
    halo = near_ref.shape[0]
    total_rows = 2 * rows
    tiles = width // LANES
    parts = 8
    depth = width // parts
    loads = []
    for part in range(parts):
        here = pl.ds(part * depth, depth)
        loads.append(
            pltpu.make_async_copy(weight_hbm.at[here], weight_ref.at[here], sems.at[part])
        )
    for load in loads:
        load.start()
    length, core = info_ref[LENGTH], info_ref[CORE]
    offset = info_ref[CHIP] * total_rows
    span = total_rows + 2 * halo
    frame = offset - halo + lax.broadcasted_iota(jnp.int32, (span, LANES), 0)
    live = (frame < length).astype(jnp.float32)
    first = halo - KERNEL // 2
    own_at = pl.ds(pl.multiple_of(halo + core * rows, 8), rows)
    partner_at = pl.ds(pl.multiple_of(halo + (1 - core) * rows, 8), rows)
    near_at = pl.ds(pl.multiple_of(core * (halo + total_rows), 8), halo)
    far_at = pl.ds(pl.multiple_of((1 - core) * (halo + total_rows), 8), halo)

    def convolve(tile, total):
        lanes = tile_lanes(tile)
        padded[near_at] = near_ref[:, lanes].astype(jnp.float32)
        padded[far_at] = far_ref[:, lanes].astype(jnp.float32)
        padded[own_at] = own_ref[:, lanes].astype(jnp.float32)
        padded[partner_at] = partner_ref[core, :, lanes].astype(jnp.float32)
        own = padded[halo : halo + total_rows]
        padded[...] = padded[...] * live
        acc = jnp.zeros((total_rows, LANES), jnp.float32)
        for tap in range(KERNEL):
            acc = acc + taps_ref[tap : tap + 1, lanes] * padded[
                first + tap : first + tap + total_rows
            ]
        grown = jnp.exp(jnp.minimum(acc, 20.0))
        product = grown * (grown + 2.0)
        value = own + acc * (product / (product + 2.0))
        residual_ref[:, lanes] = value
        return total + value

    total = lax.fori_loop(
        0, tiles, convolve, jnp.zeros((total_rows, LANES), jnp.float32), unroll=3
    )

    def store(lanes, value):
        normed_ref[:, lanes] = value.astype(jnp.bfloat16)

    row_norm(lambda tile: residual_ref[:, tile_lanes(tile)], store, tiles, mod_ref, 0, total)
    for load in loads:
        load.wait()


def project_kernel(firsts, origin, info_ref, normed_ref, weight_ref, cos_ref, sin_ref, *out_refs):
    rows = normed_ref.shape[0]
    attn = weight_ref.shape[1] // 3
    wide = 2 * LANES
    half = HEAD_DIM // 2
    cosine, sine = cos_ref[...], sin_ref[...]
    lower = lax.broadcasted_iota(jnp.int32, (rows, LANES), 1) % HEAD_DIM < half
    chip = info_ref[CHIP] if origin is None else origin
    swap = jnp.full((rows, LANES), chip & 1, jnp.int32) > 0
    for at, apart in enumerate(firsts):
        pair = (chip ^ apart) >> 1
        for part in range(3):
            start = part * attn + pair * wide
            both = jnp.dot(
                normed_ref[...],
                weight_ref[:, pl.ds(pl.multiple_of(start, wide), wide)],
                preferred_element_type=jnp.float32,
            )
            sides = []
            for side in range(2):
                value = both[:, side * LANES : (side + 1) * LANES]
                if part < 2:
                    swapped = jnp.where(
                        lower, pltpu.roll(value, LANES - half, 1), pltpu.roll(value, half, 1)
                    )
                    value = value * cosine + swapped * sine
                if part == 0:
                    value = value * HEAD_DIM**-0.5
                sides.append(value)
            out_refs[2 * at][part] = jnp.where(swap, sides[1], sides[0]).astype(jnp.bfloat16)
            out_refs[2 * at + 1][part] = jnp.where(swap, sides[0], sides[1]).astype(jnp.bfloat16)


def attend_kernel(info_ref, *refs):
    chips = len(refs) - 4
    got_refs, out_ref = refs[:chips], refs[chips]
    keys, values, queries = refs[chips + 1 :]
    _, rows, _ = got_refs[0].shape
    total = chips * rows
    length, chip = info_ref[LENGTH], info_ref[CHIP]
    low = lax.broadcasted_iota(jnp.int32, (rows, LANES), 1) < HEAD_DIM
    lane = lax.broadcasted_iota(jnp.int32, (rows, LANES), 1)
    row = lax.broadcasted_iota(jnp.int32, (rows, LANES), 0)
    zero = jnp.zeros((rows, LANES), jnp.bfloat16)
    queries[:, LANES:] = jnp.where(
        lax.broadcasted_iota(jnp.int32, (2 * total, LANES), 1) == 0, 1.0, 0.0
    ).astype(jnp.bfloat16)
    for apart, got_ref in enumerate(got_refs):
        here = slice(apart * rows, (apart + 1) * rows)
        keys[here, :LANES] = got_ref[1]
        dead = (lane == 0) & (row + (chip ^ apart) * rows >= length)
        keys[here, LANES:] = jnp.where(dead, NEGATIVE, 0.0).astype(jnp.bfloat16)
        values[here, :] = got_ref[2]
        query = got_ref[0]
        at = 2 * apart * rows
        queries[at : at + rows, :LANES] = jnp.where(low, query, zero)
        queries[at + rows : at + 2 * rows, :LANES] = jnp.where(low, zero, query)
    for first in range(0, chips, 2):
        at = 2 * first * rows
        scores = lax.dot_general(
            queries[at : at + 4 * rows, :], keys[...], (((1,), (1,)), ((), ())),
            preferred_element_type=jnp.float32,
        )
        weights = jnp.exp(scores - jnp.max(scores, axis=1, keepdims=True))
        weight_sum = jnp.sum(weights, axis=1, keepdims=True)
        mixed = jnp.dot(
            weights.astype(jnp.bfloat16), values[...], preferred_element_type=jnp.float32
        )
        mixed = mixed / weight_sum
        for side in range(2):
            base = 2 * side * rows
            out_ref[chip ^ (first + side)] = jnp.where(
                low, mixed[base : base + rows], mixed[base + rows : base + 2 * rows]
            ).astype(jnp.bfloat16)


def back_kernel(
    info_ref, got_ref, residual_ref, mod_ref, w_out_ref, w_mel_ref, keep_ref, send_ref, attended,
    after, speed,
):
    rows, width = residual_ref.shape
    tiles = width // LANES
    core = info_ref[CORE]
    for block in range(got_ref.shape[0]):
        attended[:, block * LANES : (block + 1) * LANES] = got_ref[block]
    wide = 2 * LANES
    total = jnp.zeros((rows, LANES), jnp.float32)
    for block in range(width // wide):
        lanes = slice(block * wide, (block + 1) * wide)
        branch = jnp.dot(attended[...], w_out_ref[:, lanes], preferred_element_type=jnp.float32)
        value = residual_ref[:, lanes] + mod_ref[2:3, lanes] * branch
        after[:, lanes] = value
        total = total + value[:, :LANES] + value[:, LANES:]

    def store(lanes, value):
        after[:, lanes] = value

    row_norm(lambda tile: after[:, tile_lanes(tile)], store, tiles, mod_ref, 3, total)
    speed[...] = lax.dot_general(
        after[...].astype(jnp.bfloat16), w_mel_ref[...], (((1,), (1,)), ((), ())),
        preferred_element_type=jnp.float32,
    )
    half = rows // 2
    keep_ref[...] = speed[pl.ds(pl.multiple_of(core * half, 8), half), :]
    send_ref[...] = speed[pl.ds(pl.multiple_of((1 - core) * half, 8), half), :]


def call(kernel, out_shape, inputs, scratch, limit, hbm=()):
    single = not isinstance(out_shape, tuple)
    specs = [hbm_spec() if at in hbm else vmem_spec() for at in range(1, len(inputs))]
    inputs = [
        pltpu.with_memory_space_constraint(value, pltpu.HBM) if at in hbm else value
        for at, value in enumerate(inputs)
    ]
    return pl.pallas_call(
        kernel,
        out_shape=out_shape,
        in_specs=[smem_spec()] + specs,
        out_specs=vmem_spec() if single else tuple(vmem_spec() for _ in out_shape),
        scratch_shapes=scratch,
        compiler_params=pltpu.CompilerParams(vmem_limit_bytes=limit * MIB),
    )(*inputs)


def array(shape, dtype=jnp.float32):
    return jax.ShapeDtypeStruct(shape, dtype)


def project(normed, w_qkv, tables, info, firsts, origin=None):
    shape = array((3, normed.shape[0], LANES), jnp.bfloat16)
    return call(
        functools.partial(project_kernel, tuple(firsts), origin),
        (shape,) * (2 * len(firsts)),
        (info, normed, w_qkv) + tables,
        [],
        8,
    )


def same_core(count):
    return [list(range(core, count, 2)) for core in range(2)]


def across(value, apart, count):
    return lax.ppermute(value, "seq", [(i, i ^ apart) for i in range(count)])


def to_groups(values, subs):
    rows, _ = values.shape
    grouped = values.reshape(subs, rows // subs, HEADS, HEAD_DIM).transpose(2, 0, 1, 3)
    return grouped.reshape(HEADS * subs, rows // subs, HEAD_DIM)


def from_groups(grouped, rows, subs):
    split = grouped.reshape(HEADS, subs, rows // subs, HEAD_DIM).transpose(1, 2, 0, 3)
    return split.reshape(rows, HEADS * HEAD_DIM)


def attend_blocks(queries, keys, values, live):
    groups, total, _ = queries.shape
    block = max(size for size in range(1, min(total, 1024) + 1) if total % size == 0)
    blocks = queries.reshape(groups, total // block, block, HEAD_DIM).transpose(1, 0, 2, 3)
    live = live[None, None, :]

    def one_block(query):
        scores = jnp.einsum("gqd,gkd->gqk", query, keys, preferred_element_type=jnp.float32)
        scores = jnp.where(live, scores, NEGATIVE)
        weights = jnp.exp(scores - jnp.max(scores, axis=-1, keepdims=True))
        weights = jnp.where(live, weights, 0.0)
        mixed = jnp.einsum(
            "gqk,gkd->gqd",
            weights.astype(jnp.bfloat16),
            values,
            preferred_element_type=jnp.float32,
        )
        return (mixed / jnp.sum(weights, axis=-1)[..., None]).astype(jnp.bfloat16)

    return lax.map(one_block, blocks).transpose(1, 0, 2, 3).reshape(groups, total, HEAD_DIM)


def attend_any(normed, w_qkv, tables, info, length, count):
    rows = normed.shape[0]
    chips = count // 2
    groups = HEADS * HEAD_DIM // LANES
    sent = project(normed, w_qkv, tables, info, range(0, groups, 2), 0)
    subs = max(1, chips // HEADS)
    chip = lax.axis_index("seq") >> 1
    part_rows = rows // subs

    def exchange(part):
        whole = jnp.concatenate([group[part] for group in sent], axis=1)
        return lax.all_to_all(
            to_groups(whole, subs), "seq", split_axis=0, concat_axis=1, tiled=True,
            axis_index_groups=same_core(count),
        )

    queries, keys, values = (exchange(part) for part in range(3))

    def frames_of(sub):
        start = jnp.arange(chips, dtype=jnp.int32)[:, None] * rows + sub * part_rows
        return (start + jnp.arange(part_rows, dtype=jnp.int32)[None, :]).reshape(-1)

    frames = [frames_of(chip % subs)]
    parts = [(keys, values)]
    for apart in range(1, subs):
        perm = []
        for i in range(count):
            at = i // 2
            target = at - at % subs + (at + apart) % subs
            perm.append((i, 2 * target + i % 2))
        parts.append(tuple(lax.ppermute(part, "seq", perm) for part in (keys, values)))
        frames.append(frames_of((chip - apart) % subs))
    keys = jnp.concatenate([part[0] for part in parts], axis=1)
    values = jnp.concatenate([part[1] for part in parts], axis=1)
    attended = attend_blocks(queries, keys, values, jnp.concatenate(frames) < length)
    back = lax.all_to_all(
        attended, "seq", split_axis=1, concat_axis=0, tiled=True,
        axis_index_groups=same_core(count),
    )
    return from_groups(back, rows, subs).reshape(rows, groups, LANES).transpose(1, 0, 2)


def chips_hold_groups(count):
    chips = count // 2
    return chips == HEADS * HEAD_DIM // LANES and chips >= 4 and chips & (chips - 1) == 0


def send_order(chips):
    return list(range(chips // 2, chips, 2)) + list(range(2, chips // 2, 2)) + [0]


def attend_chips(normed, w_qkv, tables, info, count):
    rows = normed.shape[0]
    chips = count // 2
    held = {}
    for first in send_order(chips):
        made = project(normed, w_qkv, tables, info, [first])
        for side in range(2):
            apart = first + side
            held[apart] = across(made[side], 2 * apart, count) if apart else made[side]
    total = chips * rows
    attended = call(
        attend_kernel,
        array((chips, rows, LANES), jnp.bfloat16),
        (info,) + tuple(held[apart] for apart in range(chips)),
        [
            VMEM((total, 2 * LANES), jnp.bfloat16),
            VMEM((total, LANES), jnp.bfloat16),
            VMEM((2 * total, 2 * LANES), jnp.bfloat16),
        ],
        24,
    )
    return lax.all_to_all(
        attended, "seq", split_axis=0, concat_axis=0, tiled=True,
        axis_index_groups=same_core(count),
    )


def per_device(
    hidden, latent, lengths, step_index, guidance, modulation, conv_kernel, w_qkv, w_out, w_mel
):
    _, rows, width = hidden.shape
    count = lax.axis_size("seq")
    chips = count // 2
    index = lax.axis_index("seq").astype(jnp.int32)
    chip, core = index >> 1, index & 1
    chip_rows = 2 * rows
    place = jnp.stack([core, chip])

    partner = across(hidden, 1, count)
    near, far = call(
        edge_kernel,
        (array((HALO, width), jnp.bfloat16),) * 2,
        (place, hidden),
        [pltpu.SemaphoreType.DMA((2,))],
        4,
        hbm=(1,),
    )
    steps = range(chips - 1)
    near = lax.ppermute(
        near, "seq",
        [(2 * m + 1, 2 * m + 2) for m in steps] + [(2 * m + 2, 2 * m + 1) for m in steps],
    )
    far = lax.ppermute(
        far, "seq",
        [(2 * m + 1, 2 * m + 3) for m in steps] + [(2 * m + 2, 2 * m) for m in steps],
    )
    own, taps, mods = call(
        stage_kernel,
        (
            array((rows, width), jnp.bfloat16),
            array(conv_kernel.shape),
            array(modulation.shape),
        ),
        (place, hidden, conv_kernel, modulation),
        [pltpu.SemaphoreType.DMA((3,))],
        4,
        hbm=(1, 2, 3),
    )
    info = jnp.stack([core, chip, lengths[0]])
    tables = rotary_tables(chip * chip_rows + jnp.arange(chip_rows, dtype=jnp.int32))
    residual, normed, weight = call(
        front_kernel,
        (
            array((chip_rows, width)),
            array((chip_rows, width), jnp.bfloat16),
            array(w_qkv.shape, jnp.bfloat16),
        ),
        (info, own, partner, near, far, taps, mods, w_qkv),
        [VMEM((chip_rows + 2 * HALO, LANES), jnp.float32), pltpu.SemaphoreType.DMA((8,))],
        8,
        hbm=(7,),
    )
    if chips_hold_groups(count):
        back = attend_chips(normed, weight, tables, info, count)
    else:
        back = attend_any(normed, weight, tables, info, lengths[0], count)
    mels = w_mel.shape[1]
    residual, w_mel = call(
        fetch_kernel,
        (array(residual.shape), array((mels, width), jnp.bfloat16)),
        (place, residual, w_mel.T),
        [pltpu.SemaphoreType.DMA((2,))],
        4,
        hbm=(1, 2),
    )
    keep, send = call(
        back_kernel,
        (array((rows, mels)),) * 2,
        (info, back, residual, mods, w_out, w_mel),
        [
            VMEM((chip_rows, HEADS * HEAD_DIM), jnp.bfloat16),
            VMEM((chip_rows, width), jnp.float32),
            VMEM((chip_rows, mels), jnp.float32),
        ],
        12,
    )
    other = across(send, 1, count)
    first = jnp.where(core == 0, keep, other)
    second = jnp.where(core == 0, other, keep)
    guided = first + guidance[0] * (first - second)
    live = index * rows + jnp.arange(rows, dtype=jnp.int32) < lengths[0]
    velocity = jnp.where(live[:, None], guided, 0.0)
    progress = step_index[0].astype(jnp.float32) / STEPS
    time_now = 1.0 - jnp.cos(0.5 * jnp.pi * progress)
    return (velocity, latent + (1.0 - time_now) * velocity)


def solution(mesh):
    return jax.shard_map(
        per_device,
        mesh=mesh,
        in_specs=(
            P(None, ("clip", "seq"), None),
            P(("clip", "seq"), None),
            P("clip"),
            P(),
            P(),
            P(),
            P(),
            P(),
            P(),
            P(),
        ),
        out_specs=(P(("clip", "seq"), None), P(("clip", "seq"), None)),
        check_vma=False,
    )
```

profile of v0, /device:TPU:0, one launch (start us, length us, event | category | flops | bytes accessed | tf_op | source)
XLA Modules:
  0.0 62.7 jit_solution(16564008621911767129)
XLA Ops:
  0.6 0.6 collective-permute-start
  1.2 0.1 pad_add_fusion.1.info_ref
  1.3 1.4 %shard_map.114 = (bf16[16,1536]{1,0:T(8,128)(2,1)S(1)}, bf16[16,1536]{1,0:T(8,128)(2,1)S(1)}) custom-call(s32[2]{0:T(128)S(1)} %pad_add_fusion.1.info_ref, bf16[2,56,1536]{2,1,0:T(8,128)(2,1)} %hidden_hbm.3), custom_call_target="tpu_custom_call" | custom-call | tf_op jit(solution)/shard_map/pallas_call | solution.py:283
  2.7 0.7 %collective-permute-start.1 = (bf16[16,1536]{1,0:T(8,128)(2,1)S(1)}, bf16[16,1536]{1,0:T(8,128)(2,1)S(1)}, u32[]{:S(2)}, u32[]{:S(2)}) collective-permute-start(bf16[16,1536]{1,0:T(8,128)(2,1)S(1)} %get-tuple-element.23), channel_id=1, source_target_pairs={{1,2},{3,4},{5,6},{7,8},{9,10},{11,12},{13,14},{2,1},{4,3},{6,5},{... | collective-permute-start | bytes 147464 | tf_op jit(solution)/shard_map/ppermute | solution.py:448
  3.3 1.3 %collective-permute-start.2 = (bf16[16,1536]{1,0:T(8,128)(2,1)S(1)}, bf16[16,1536]{1,0:T(8,128)(2,1)S(1)}, u32[]{:S(2)}, u32[]{:S(2)}) collective-permute-start(bf16[16,1536]{1,0:T(8,128)(2,1)S(1)} %get-tuple-element.24), channel_id=1, source_target_pairs={{1,3},{3,5},{5,7},{7,9},{9,11},{11,13},{13,15},{2,0},{4,2},{6,4},{... | collective-permute-start | bytes 147464 | tf_op jit(solution)/shard_map/ppermute | solution.py:452
  5.3 0.3 fusion
  5.6 0.1 pad_add_fusion.info_ref
  5.7 1.6 %shard_map.113 = (bf16[56,1536]{1,0:T(8,128)(2,1)S(1)}, f32[31,1536]{1,0:T(8,128)S(1)}, f32[5,1536]{1,0:T(8,128)S(1)}) custom-call(s32[2]{0:T(128)S(1)} %pad_add_fusion.1.info_ref, bf16[2,56,1536]{2,1,0:T(8,128)(2,1)} %hidden_hbm.3, f32[31,1536]{1,0:T(8,128)} %taps_hbm.1, f32[5,1536]{1,0:T(8,128)} %mod_hbm.1), custom_call_target="tpu_custom_call" | custom-call | tf_op jit(solution)/shard_map/pallas_call | solution.py:283
  7.3 0.0 collective-permute-done.1.near_ref
  7.3 3.8 %collective-permute-done.2.far_ref = bf16[16,1536]{1,0:T(8,128)(2,1)S(1)} collective-permute-done((bf16[16,1536]{1,0:T(8,128)(2,1)S(1)}, bf16[16,1536]{1,0:T(8,128)(2,1)S(1)}, u32[]{:S(2)}, u32[]{:S(2)}) %collective-permute-start.2) | collective-permute-done | bytes 49184 | tf_op jit(solution)/shard_map/ppermute | solution.py:452
  11.1 0.0 collective-permute-done.partner_ref
  11.1 4.3 %shard_map.115 = (f32[112,1536]{1,0:T(8,128)S(1)}, bf16[112,1536]{1,0:T(8,128)(2,1)S(1)}, bf16[1536,3072]{1,0:T(8,128)(2,1)S(1)}) custom-call(s32[3]{0:T(128)S(1)} %pad_add_fusion.info_ref, bf16[56,1536]{1,0:T(8,128)(2,1)S(1)} %get-tuple-element.22.own_ref, bf16[2,56,1536]{2,1,0:T(8,128)(2,1)S(1)} %collective-permute-done.partner_ref, ...), custom_call_target="tpu_custom_call" | custom-call | tf_op jit(solution)/shard_map/pallas_call | solution.py:283
  15.4 0.0 copy-start.3
  15.4 1.2 %shard_map.119 = (bf16[3,112,128]{2,1,0:T(8,128)(2,1)S(1)}, bf16[3,112,128]{2,1,0:T(8,128)(2,1)S(1)}) custom-call(s32[3]{0:T(128)S(1)} %pad_add_fusion.info_ref, bf16[112,1536]{1,0:T(8,128)(2,1)S(1)} %get-tuple-element.27.normed_ref, bf16[1536,3072]{1,0:T(8,128)(2,1)S(1)} %get-tuple-element.28.weight_ref, f32[112,128]{1,0:T(8,128)S(1)} %get-tuple-element.45.cos_ref, ...), custom_call_target="tpu_custom_call" | custom-call | tf_op jit(solution)/shard_map/pallas_call | solution.py:283
  16.6 6.1 %collective-permute-start.8 = (bf16[3,112,128]{2,1,0:T(8,128)(2,1)S(1)}, bf16[3,112,128]{2,1,0:T(8,128)(2,1)S(1)}, u32[]{:S(2)}, u32[]{:S(2)}) collective-permute-start(bf16[3,112,128]{2,1,0:T(8,128)(2,1)S(1)} %get-tuple-element.35), channel_id=1, source_target_pairs={{0,12},{1,13},{2,14},{3,15},{4,8},{5,9},{6,10},{7,11},{8,4},{9,5},... | collective-permute-start | bytes 258056 | tf_op jit(solution)/shard_map/ppermute | solution.py:313
  22.8 0.3 collective-permute-start.9
  23.1 1.2 %shard_map.118 = (bf16[3,112,128]{2,1,0:T(8,128)(2,1)S(1)}, bf16[3,112,128]{2,1,0:T(8,128)(2,1)S(1)}) custom-call(s32[3]{0:T(128)S(1)} %pad_add_fusion.info_ref, bf16[112,1536]{1,0:T(8,128)(2,1)S(1)} %get-tuple-element.27.normed_ref, bf16[1536,3072]{1,0:T(8,128)(2,1)S(1)} %get-tuple-element.28.weight_ref, f32[112,128]{1,0:T(8,128)S(1)} %get-tuple-element.45.cos_ref, ...), custom_call_target="tpu_custom_call" | custom-call | tf_op jit(solution)/shard_map/pallas_call | solution.py:283
  24.2 0.0 copy-done.3
  24.2 0.0 copy-start
  24.2 1.2 %shard_map.117 = (bf16[3,112,128]{2,1,0:T(8,128)(2,1)S(1)}, bf16[3,112,128]{2,1,0:T(8,128)(2,1)S(1)}) custom-call(s32[3]{0:T(128)S(1)} %pad_add_fusion.info_ref, bf16[112,1536]{1,0:T(8,128)(2,1)S(1)} %get-tuple-element.27.normed_ref, bf16[1536,3072]{1,0:T(8,128)(2,1)S(1)} %get-tuple-element.28.weight_ref, f32[112,128]{1,0:T(8,128)S(1)} %get-tuple-element.45.cos_ref, ...), custom_call_target="tpu_custom_call" | custom-call | tf_op jit(solution)/shard_map/pallas_call | solution.py:283
  25.4 0.0 copy-start.6
  25.5 1.2 %shard_map.116 = (bf16[3,112,128]{2,1,0:T(8,128)(2,1)S(1)}, bf16[3,112,128]{2,1,0:T(8,128)(2,1)S(1)}) custom-call(s32[3]{0:T(128)S(1)} %pad_add_fusion.info_ref, bf16[112,1536]{1,0:T(8,128)(2,1)S(1)} %get-tuple-element.27.normed_ref, bf16[1536,3072]{1,0:T(8,128)(2,1)S(1)} %get-tuple-element.28.weight_ref, f32[112,128]{1,0:T(8,128)S(1)} %get-tuple-element.45.cos_ref, ...), custom_call_target="tpu_custom_call" | custom-call | tf_op jit(solution)/shard_map/pallas_call | solution.py:283
  26.6 1.2 %collective-permute-start.6 = (bf16[3,112,128]{2,1,0:T(8,128)(2,1)S(1)}, bf16[3,112,128]{2,1,0:T(8,128)(2,1)S(1)}, u32[]{:S(2)}, u32[]{:S(2)}) collective-permute-start(bf16[3,112,128]{2,1,0:T(8,128)(2,1)S(1)} %get-tuple-element.33), channel_id=1, source_target_pairs={{0,8},{1,9},{2,10},{3,11},{4,12},{5,13},{6,14},{7,15},{8,0},{9,1},... | collective-permute-start | bytes 258056 | tf_op jit(solution)/shard_map/ppermute | solution.py:313
  27.9 2.4 %collective-permute-start.7 = (bf16[3,112,128]{2,1,0:T(8,128)(2,1)S(1)}, bf16[3,112,128]{2,1,0:T(8,128)(2,1)S(1)}, u32[]{:S(2)}, u32[]{:S(2)}) collective-permute-start(bf16[3,112,128]{2,1,0:T(8,128)(2,1)S(1)} %get-tuple-element.34), channel_id=1, source_target_pairs={{0,10},{1,11},{2,8},{3,9},{4,14},{5,15},{6,12},{7,13},{8,2},{9,3},... | collective-permute-start | bytes 258056 | tf_op jit(solution)/shard_map/ppermute | solution.py:313
  30.3 1.5 %collective-permute-start.4 = (bf16[3,112,128]{2,1,0:T(8,128)(2,1)S(1)}, bf16[3,112,128]{2,1,0:T(8,128)(2,1)S(1)}, u32[]{:S(2)}, u32[]{:S(2)}) collective-permute-start(bf16[3,112,128]{2,1,0:T(8,128)(2,1)S(1)} %get-tuple-element.31), channel_id=1, source_target_pairs={{0,4},{1,5},{2,6},{3,7},{4,0},{5,1},{6,2},{7,3},{8,12},{9,13},{10,... | collective-permute-start | bytes 258056 | tf_op jit(solution)/shard_map/ppermute | solution.py:313
  31.8 0.0 collective-permute-done.8.refs_6_
  31.8 0.7 %collective-permute-start.5 = (bf16[3,112,128]{2,1,0:T(8,128)(2,1)S(1)}, bf16[3,112,128]{2,1,0:T(8,128)(2,1)S(1)}, u32[]{:S(2)}, u32[]{:S(2)}) collective-permute-start(bf16[3,112,128]{2,1,0:T(8,128)(2,1)S(1)} %get-tuple-element.32), channel_id=1, source_target_pairs={{0,6},{1,7},{2,4},{3,5},{4,2},{5,3},{6,0},{7,1},{8,14},{9,15},{10,... | collective-permute-start | bytes 258056 | tf_op jit(solution)/shard_map/ppermute | solution.py:313
  32.5 0.0 collective-permute-done.9.refs_7_
  32.5 1.2 %collective-permute-start.3 = (bf16[3,112,128]{2,1,0:T(8,128)(2,1)S(1)}, bf16[3,112,128]{2,1,0:T(8,128)(2,1)S(1)}, u32[]{:S(2)}, u32[]{:S(2)}) collective-permute-start(bf16[3,112,128]{2,1,0:T(8,128)(2,1)S(1)} %get-tuple-element.30), channel_id=1, source_target_pairs={{0,2},{1,3},{2,0},{3,1},{4,6},{5,7},{6,4},{7,5},{8,10},{9,11},{10,... | collective-permute-start | bytes 258056 | tf_op jit(solution)/shard_map/ppermute | solution.py:313
  33.8 1.1 %collective-permute-done.6.refs_4_ = bf16[3,112,128]{2,1,0:T(8,128)(2,1)S(1)} collective-permute-done((bf16[3,112,128]{2,1,0:T(8,128)(2,1)S(1)}, bf16[3,112,128]{2,1,0:T(8,128)(2,1)S(1)}, u32[]{:S(2)}, u32[]{:S(2)}) %collective-permute-start.6) | collective-permute-done | bytes 86048 | tf_op jit(solution)/shard_map/ppermute | solution.py:313
  34.9 3.1 %collective-permute-done.7.refs_5_ = bf16[3,112,128]{2,1,0:T(8,128)(2,1)S(1)} collective-permute-done((bf16[3,112,128]{2,1,0:T(8,128)(2,1)S(1)}, bf16[3,112,128]{2,1,0:T(8,128)(2,1)S(1)}, u32[]{:S(2)}, u32[]{:S(2)}) %collective-permute-start.7) | collective-permute-done | bytes 86048 | tf_op jit(solution)/shard_map/ppermute | solution.py:313
  38.0 0.0 collective-permute-done.4.refs_2_
  38.0 1.3 %collective-permute-done.5.refs_3_ = bf16[3,112,128]{2,1,0:T(8,128)(2,1)S(1)} collective-permute-done((bf16[3,112,128]{2,1,0:T(8,128)(2,1)S(1)}, bf16[3,112,128]{2,1,0:T(8,128)(2,1)S(1)}, u32[]{:S(2)}, u32[]{:S(2)}) %collective-permute-start.5) | collective-permute-done | bytes 86048 | tf_op jit(solution)/shard_map/ppermute | solution.py:313
  39.3 0.4 collective-permute-done.3.refs_1_
  39.7 4.3 %shard_map.120 = bf16[8,112,128]{2,1,0:T(8,128)(2,1)} custom-call(s32[3]{0:T(128)S(1)} %pad_add_fusion.info_ref, bf16[3,112,128]{2,1,0:T(8,128)(2,1)S(1)} %get-tuple-element.29.refs_0_, bf16[3,112,128]{2,1,0:T(8,128)(2,1)S(1)} %collective-permute-done.3.refs_1_, bf16[3,112,128]{2,1,0:T(8,128)(2,1)S(1)} %collective-permute-done.4.refs_2_, ...), custom_call_target="tpu_custom_call" | custom-call | tf_op jit(solution)/shard_map/pallas_call | solution.py:283
  44.0 4.5 %all-to-all-start = ((bf16[8,112,128]{2,1,0:T(8,128)(2,1)}), bf16[8,112,128]{2,1,0:T(8,128)(2,1)S(1)}, u32[]{:S(2)}, u32[]{:S(2)}) async-start(bf16[8,112,128]{2,1,0:T(8,128)(2,1)} %shard_map.120), calls=%async_computation | async-start | bytes 458752 | tf_op jit(solution)/shard_map/all_to_all | solution.py:421
  48.5 1.7 %shard_map.121 = (f32[112,1536]{1,0:T(8,128)S(1)}, bf16[100,1536]{1,0:T(8,128)(2,1)S(1)}) custom-call(s32[2]{0:T(128)S(1)} %pad_add_fusion.1.info_ref, f32[112,1536]{1,0:T(8,128)} %copy-done.3, bf16[100,1536]{1,0:T(8,128)(2,1)} %bitcast.8), custom_call_target="tpu_custom_call" | custom-call | tf_op jit(solution)/shard_map/pallas_call | solution.py:283
  50.2 0.0 copy-start.1
  50.2 0.8 %copy-done.1 = f32[112,1536]{1,0:T(8,128)} copy-done((f32[112,1536]{1,0:T(8,128)}, f32[112,1536]{1,0:T(8,128)S(1)}, u32[]{:S(2)}) %copy-start.1) | copy-done | bytes 688152
  51.1 0.7 %copy-done.4 = bf16[100,1536]{1,0:T(8,128)(2,1)} copy-done((bf16[100,1536]{1,0:T(8,128)(2,1)}, bf16[100,1536]{1,0:T(8,128)(2,1)S(1)}, u32[]{:S(2)}) %copy-start.4) | copy-done | bytes 307224
  51.8 4.7 %all-to-all-done.got_ref = bf16[8,112,128]{2,1,0:T(8,128)(2,1)S(1)} async-done(((bf16[8,112,128]{2,1,0:T(8,128)(2,1)}), bf16[8,112,128]{2,1,0:T(8,128)(2,1)S(1)}, u32[]{:S(2)}, u32[]{:S(2)}) %all-to-all-start) | async-done | bytes 229408 | tf_op jit(solution)/shard_map/all_to_all | solution.py:421
  56.5 1.1 %copy-done.2 = f32[112,1536]{1,0:T(8,128)S(1)} copy-done((f32[112,1536]{1,0:T(8,128)S(1)}, f32[112,1536]{1,0:T(8,128)}, u32[]{:S(2)}) %copy-start.2) | copy-done | bytes 688152
  57.6 1.0 %copy-done.5 = bf16[100,1536]{1,0:T(8,128)(2,1)S(1)} copy-done((bf16[100,1536]{1,0:T(8,128)(2,1)S(1)}, bf16[100,1536]{1,0:T(8,128)(2,1)}, u32[]{:S(2)}) %copy-start.5) | copy-done | bytes 307224
  58.5 2.0 %shard_map.122 = (f32[56,100]{1,0:T(8,128)S(1)}, f32[56,100]{1,0:T(8,128)S(1)}) custom-call(s32[3]{0:T(128)S(1)} %pad_add_fusion.info_ref, bf16[8,112,128]{2,1,0:T(8,128)(2,1)S(1)} %all-to-all-done.got_ref, f32[112,1536]{1,0:T(8,128)S(1)} %copy-done.2, f32[5,1536]{1,0:T(8,128)S(1)} %get-tuple-element.26.mod_ref, bf16[1024,1536]{1,0:T(8,128)(2,1)S(1)} %copy-done, ...), custom_call_target="tpu_custom_call" | custom-call | tf_op jit(solution)/shard_map/pallas_call | solution.py:283
  60.5 0.1 collective-permute-start.10
  62.0 0.0 collective-permute-done.10
  62.0 0.0 copy-done.6
  62.0 0.7 %multiply_add_fusion = (f32[56,100]{1,0:T(8,128)}, f32[56,100]{1,0:T(8,128)}) fusion(f32[56,100]{1,0:T(8,128)S(1)} %copy-done.6, f32[]{:T(128)} %bitcast.5, f32[56,100]{1,0:T(8,128)S(1)} %collective-permute-done.10, f32[56,100]{1,0:T(8,128)S(1)} %get-tuple-element.40, f32[]{:T(128)} %bitcast.7, pred[]{:T(512)S(6)} %eq.7, pred[56]{0:T(512)(128)(4,1)S(1)} %add_compare_fusion), kind=kLoop, calls=%fused_computation.3 | loop fusion | flops 44800 | bytes 112065 | tf_op jit(solution)/shard_map/add | solution.py:514
  (7 shorter events, 0.0 us)
Async XLA Ops:
  0.6 10.5 %collective-permute-start = (bf16[2,56,1536]{2,1,0:T(8,128)(2,1)}, bf16[2,56,1536]{2,1,0:T(8,128)(2,1)S(1)}, u32[]{:S(2)}, u32[]{:S(2)}) collective-permute-start(bf16[2,56,1536]{2,1,0:T(8,128)(2,1)} %hidden_hbm.3), channel_id=1, source_target_pairs={{0,1},{1,0},{2,3},{3,2},{4,5},{5,4},{6,7},{7,6},{8,9},{9,8},{10,11... | collective-permute-start | bytes 1032200 | tf_op jit(solution)/shard_map/ppermute | solution.py:313
  2.7 4.6 %collective-permute-start.1 = (bf16[16,1536]{1,0:T(8,128)(2,1)S(1)}, bf16[16,1536]{1,0:T(8,128)(2,1)S(1)}, u32[]{:S(2)}, u32[]{:S(2)}) collective-permute-start(bf16[16,1536]{1,0:T(8,128)(2,1)S(1)} %get-tuple-element.23), channel_id=1, source_target_pairs={{1,2},{3,4},{5,6},{7,8},{9,10},{11,12},{13,14},{2,1},{4,3},{6,5},{... | collective-permute-start | bytes 147464 | tf_op jit(solution)/shard_map/ppermute | solution.py:448
  3.3 7.8 %collective-permute-start.2 = (bf16[16,1536]{1,0:T(8,128)(2,1)S(1)}, bf16[16,1536]{1,0:T(8,128)(2,1)S(1)}, u32[]{:S(2)}, u32[]{:S(2)}) collective-permute-start(bf16[16,1536]{1,0:T(8,128)(2,1)S(1)} %get-tuple-element.24), channel_id=1, source_target_pairs={{1,3},{3,5},{5,7},{7,9},{9,11},{11,13},{13,15},{2,0},{4,2},{6,4},{... | collective-permute-start | bytes 147464 | tf_op jit(solution)/shard_map/ppermute | solution.py:452
  15.4 8.8 %copy-start.3 = (f32[112,1536]{1,0:T(8,128)}, f32[112,1536]{1,0:T(8,128)S(1)}, u32[]{:S(2)}) copy-start(f32[112,1536]{1,0:T(8,128)S(1)} %get-tuple-element.37.residual_hbm) | copy-start | bytes 2064388
  16.6 15.2 %collective-permute-start.8 = (bf16[3,112,128]{2,1,0:T(8,128)(2,1)S(1)}, bf16[3,112,128]{2,1,0:T(8,128)(2,1)S(1)}, u32[]{:S(2)}, u32[]{:S(2)}) collective-permute-start(bf16[3,112,128]{2,1,0:T(8,128)(2,1)S(1)} %get-tuple-element.35), channel_id=1, source_target_pairs={{0,12},{1,13},{2,14},{3,15},{4,8},{5,9},{6,10},{7,11},{8,4},{9,5},... | collective-permute-start | bytes 258056 | tf_op jit(solution)/shard_map/ppermute | solution.py:313
  22.8 9.8 %collective-permute-start.9 = (bf16[3,112,128]{2,1,0:T(8,128)(2,1)S(1)}, bf16[3,112,128]{2,1,0:T(8,128)(2,1)S(1)}, u32[]{:S(2)}, u32[]{:S(2)}) collective-permute-start(bf16[3,112,128]{2,1,0:T(8,128)(2,1)S(1)} %get-tuple-element.36), channel_id=1, source_target_pairs={{0,14},{1,15},{2,12},{3,13},{4,10},{5,11},{6,8},{7,9},{8,6},{9,7},... | collective-permute-start | bytes 258056 | tf_op jit(solution)/shard_map/ppermute | solution.py:313
  24.2 32.2 %copy-start = (bf16[1024,1536]{1,0:T(8,128)(2,1)S(1)}, bf16[1024,1536]{1,0:T(8,128)(2,1)}, u32[]{:S(2)}) copy-start(bf16[1024,1536]{1,0:T(8,128)(2,1)} %w_out_ref.1) | copy-start | bytes 9437188
  25.4 36.6 %copy-start.6 = (f32[56,100]{1,0:T(8,128)S(1)}, f32[56,100]{1,0:T(8,128)}, u32[]{:S(2)}) copy-start(f32[56,100]{1,0:T(8,128)} %param.11) | copy-start | bytes 67204
  26.6 8.3 %collective-permute-start.6 = (bf16[3,112,128]{2,1,0:T(8,128)(2,1)S(1)}, bf16[3,112,128]{2,1,0:T(8,128)(2,1)S(1)}, u32[]{:S(2)}, u32[]{:S(2)}) collective-permute-start(bf16[3,112,128]{2,1,0:T(8,128)(2,1)S(1)} %get-tuple-element.33), channel_id=1, source_target_pairs={{0,8},{1,9},{2,10},{3,11},{4,12},{5,13},{6,14},{7,15},{8,0},{9,1},... | collective-permute-start | bytes 258056 | tf_op jit(solution)/shard_map/ppermute | solution.py:313
  27.9 10.1 %collective-permute-start.7 = (bf16[3,112,128]{2,1,0:T(8,128)(2,1)S(1)}, bf16[3,112,128]{2,1,0:T(8,128)(2,1)S(1)}, u32[]{:S(2)}, u32[]{:S(2)}) collective-permute-start(bf16[3,112,128]{2,1,0:T(8,128)(2,1)S(1)} %get-tuple-element.34), channel_id=1, source_target_pairs={{0,10},{1,11},{2,8},{3,9},{4,14},{5,15},{6,12},{7,13},{8,2},{9,3},... | collective-permute-start | bytes 258056 | tf_op jit(solution)/shard_map/ppermute | solution.py:313
  30.3 7.7 %collective-permute-start.4 = (bf16[3,112,128]{2,1,0:T(8,128)(2,1)S(1)}, bf16[3,112,128]{2,1,0:T(8,128)(2,1)S(1)}, u32[]{:S(2)}, u32[]{:S(2)}) collective-permute-start(bf16[3,112,128]{2,1,0:T(8,128)(2,1)S(1)} %get-tuple-element.31), channel_id=1, source_target_pairs={{0,4},{1,5},{2,6},{3,7},{4,0},{5,1},{6,2},{7,3},{8,12},{9,13},{10,... | collective-permute-start | bytes 258056 | tf_op jit(solution)/shard_map/ppermute | solution.py:313
  31.8 7.5 %collective-permute-start.5 = (bf16[3,112,128]{2,1,0:T(8,128)(2,1)S(1)}, bf16[3,112,128]{2,1,0:T(8,128)(2,1)S(1)}, u32[]{:S(2)}, u32[]{:S(2)}) collective-permute-start(bf16[3,112,128]{2,1,0:T(8,128)(2,1)S(1)} %get-tuple-element.32), channel_id=1, source_target_pairs={{0,6},{1,7},{2,4},{3,5},{4,2},{5,3},{6,0},{7,1},{8,14},{9,15},{10,... | collective-permute-start | bytes 258056 | tf_op jit(solution)/shard_map/ppermute | solution.py:313
  32.5 7.1 %collective-permute-start.3 = (bf16[3,112,128]{2,1,0:T(8,128)(2,1)S(1)}, bf16[3,112,128]{2,1,0:T(8,128)(2,1)S(1)}, u32[]{:S(2)}, u32[]{:S(2)}) collective-permute-start(bf16[3,112,128]{2,1,0:T(8,128)(2,1)S(1)} %get-tuple-element.30), channel_id=1, source_target_pairs={{0,2},{1,3},{2,0},{3,1},{4,6},{5,7},{6,4},{7,5},{8,10},{9,11},{10,... | collective-permute-start | bytes 258056 | tf_op jit(solution)/shard_map/ppermute | solution.py:313
  44.0 12.5 %all-to-all-start = ((bf16[8,112,128]{2,1,0:T(8,128)(2,1)}), bf16[8,112,128]{2,1,0:T(8,128)(2,1)S(1)}, u32[]{:S(2)}, u32[]{:S(2)}) async-start(bf16[8,112,128]{2,1,0:T(8,128)(2,1)} %shard_map.120), calls=%async_computation | async-start | bytes 458752 | tf_op jit(solution)/shard_map/all_to_all | solution.py:421
  50.2 0.8 %copy-start.1 = (f32[112,1536]{1,0:T(8,128)}, f32[112,1536]{1,0:T(8,128)S(1)}, u32[]{:S(2)}) copy-start(f32[112,1536]{1,0:T(8,128)S(1)} %get-tuple-element.38.residual_ref) | copy-start | bytes 2064388
  51.1 0.7 %copy-start.4 = (bf16[100,1536]{1,0:T(8,128)(2,1)}, bf16[100,1536]{1,0:T(8,128)(2,1)S(1)}, u32[]{:S(2)}) copy-start(bf16[100,1536]{1,0:T(8,128)(2,1)S(1)} %get-tuple-element.39.w_mel_ref) | copy-start | bytes 921604
  56.5 1.1 %copy-start.2 = (f32[112,1536]{1,0:T(8,128)S(1)}, f32[112,1536]{1,0:T(8,128)}, u32[]{:S(2)}) copy-start(f32[112,1536]{1,0:T(8,128)} %copy-done.1) | copy-start | bytes 2064388
  57.6 1.0 %copy-start.5 = (bf16[100,1536]{1,0:T(8,128)(2,1)S(1)}, bf16[100,1536]{1,0:T(8,128)(2,1)}, u32[]{:S(2)}) copy-start(bf16[100,1536]{1,0:T(8,128)(2,1)} %copy-done.4) | copy-start | bytes 921604
  60.5 1.5 %collective-permute-start.10 = (f32[56,100]{1,0:T(8,128)S(1)}, f32[56,100]{1,0:T(8,128)S(1)}, u32[]{:S(2)}, u32[]{:S(2)}) collective-permute-start(f32[56,100]{1,0:T(8,128)S(1)} %get-tuple-element.41), channel_id=1, source_target_pairs={{0,1},{1,0},{2,3},{3,2},{4,5},{5,4},{6,7},{7,6},{8,9},{9,8},{10,11... | collective-permute-start | bytes 67208 | tf_op jit(solution)/shard_map/ppermute | solution.py:313
where the time goes:
time: 63.2 us; the launch traced here: 62.7 us
  starting transfers between devices  20.7 us (33%)
  Pallas kernels  20 us (32%)
  waiting for transfers between devices  14.3 us (23%)
  local copies, waits for them, and re-layouts  3.67 us (6%)
  between operations  2.85 us (5%)
  other arithmetic  1.16 us (2%)
    pallas_call x10, Pallas kernels, call(): pl.pallas_call(kernel, out_shape=out_shape, in_specs=[smem_spec()] + spec...  20 us
    ppermute x9, starting transfers between devices, across(): return lax.ppermute(value, 'seq', [(i, i ^ apart) for i in range(count)])  14.2 us
    ppermute x9, waiting for transfers between devices, across(): return lax.ppermute(value, 'seq', [(i, i ^ apart) for i in range(count)])  5.86 us
    all_to_all x1, waiting for transfers between devices, attend_chips(): lax.all_to_all(attended, 'seq', split_axis=0, concat_axis=0, tiled=True,...  4.67 us
    all_to_all x1, starting transfers between devices, attend_chips(): lax.all_to_all(attended, 'seq', split_axis=0, concat_axis=0, tiled=True,...  4.49 us
    ppermute x1, waiting for transfers between devices, per_device(): lax.ppermute(far, 'seq', [(2 * m + 1, 2 * m + 3) for m in steps] + [(2 *...  3.81 us
    unnamed x14, local copies, waits for them, and re-layouts  3.67 us
    ppermute x1, starting transfers between devices, per_device(): lax.ppermute(far, 'seq', [(2 * m + 1, 2 * m + 3) for m in steps] + [(2 *...  1.29 us
  transfers between devices with their start and end apart: 12, of which 6 were waited for; matrix products, arithmetic and copies ran while one was open for 1% of the time, Pallas kernels for 13%

commit v1 on v0

--- a/solution.py
+++ b/solution.py
@@ -82,14 +82,6 @@
         copy.wait()
 
 
-def edge_kernel(info_ref, hidden_hbm, near_ref, far_ref, sems):
-    core = info_ref[CORE]
-    edge = pl.ds(pl.multiple_of(core * (hidden_hbm.shape[1] - HALO), 8), HALO)
-    run_copies(
-        [(hidden_hbm.at[1 - core, edge], near_ref), (hidden_hbm.at[core, edge], far_ref)], sems
-    )
-
-
 def stage_kernel(info_ref, hidden_hbm, taps_hbm, mod_hbm, own_ref, taps_ref, mod_ref, sems):
     run_copies(
         [
@@ -99,11 +91,6 @@
         ],
         sems,
     )
-
-
-def fetch_kernel(info_ref, residual_hbm, w_mel_hbm, residual_ref, w_mel_ref, sems):
-    del info_ref
-    run_copies([(residual_hbm, residual_ref), (w_mel_hbm, w_mel_ref)], sems)
 
 
 def front_kernel(
@@ -199,34 +186,35 @@
             out_refs[2 * at + 1][part] = jnp.where(swap, sides[0], sides[1]).astype(jnp.bfloat16)
 
 
-def attend_kernel(info_ref, *refs):
-    chips = len(refs) - 4
-    got_refs, out_ref = refs[:chips], refs[chips]
-    keys, values, queries = refs[chips + 1 :]
+def gather_keys(info_ref, got_refs, keys, values):
     _, rows, _ = got_refs[0].shape
-    total = chips * rows
     length, chip = info_ref[LENGTH], info_ref[CHIP]
-    low = lax.broadcasted_iota(jnp.int32, (rows, LANES), 1) < HEAD_DIM
     lane = lax.broadcasted_iota(jnp.int32, (rows, LANES), 1)
     row = lax.broadcasted_iota(jnp.int32, (rows, LANES), 0)
-    zero = jnp.zeros((rows, LANES), jnp.bfloat16)
-    queries[:, LANES:] = jnp.where(
-        lax.broadcasted_iota(jnp.int32, (2 * total, LANES), 1) == 0, 1.0, 0.0
-    ).astype(jnp.bfloat16)
     for apart, got_ref in enumerate(got_refs):
         here = slice(apart * rows, (apart + 1) * rows)
         keys[here, :LANES] = got_ref[1]
         dead = (lane == 0) & (row + (chip ^ apart) * rows >= length)
         keys[here, LANES:] = jnp.where(dead, NEGATIVE, 0.0).astype(jnp.bfloat16)
         values[here, :] = got_ref[2]
-        query = got_ref[0]
-        at = 2 * apart * rows
-        queries[at : at + rows, :LANES] = jnp.where(low, query, zero)
-        queries[at + rows : at + 2 * rows, :LANES] = jnp.where(low, zero, query)
-    for first in range(0, chips, 2):
-        at = 2 * first * rows
+
+
+def attend_rows(query_refs, keys, values, out_ref, queries):
+    _, rows, _ = query_refs[0].shape
+    low = lax.broadcasted_iota(jnp.int32, (rows, LANES), 1) < HEAD_DIM
+    zero = jnp.zeros((rows, LANES), jnp.bfloat16)
+    queries[:, LANES:] = jnp.where(
+        lax.broadcasted_iota(jnp.int32, (queries.shape[0], LANES), 1) == 0, 1.0, 0.0
+    ).astype(jnp.bfloat16)
+    for at, query_ref in enumerate(query_refs):
+        query = query_ref[0]
+        base = 2 * at * rows
+        queries[base : base + rows, :LANES] = jnp.where(low, query, zero)
+        queries[base + rows : base + 2 * rows, :LANES] = jnp.where(low, zero, query)
+    for first in range(0, len(query_refs), 2):
+        base = 2 * first * rows
         scores = lax.dot_general(
-            queries[at : at + 4 * rows, :], keys[...], (((1,), (1,)), ((), ())),
+            queries[base : base + 4 * rows, :], keys[...], (((1,), (1,)), ((), ())),
             preferred_element_type=jnp.float32,
         )
         weights = jnp.exp(scores - jnp.max(scores, axis=1, keepdims=True))
@@ -237,35 +225,69 @@
         mixed = mixed / weight_sum
         for side in range(2):
             base = 2 * side * rows
-            out_ref[chip ^ (first + side)] = jnp.where(
+            out_ref[first + side] = jnp.where(
                 low, mixed[base : base + rows], mixed[base + rows : base + 2 * rows]
             ).astype(jnp.bfloat16)
 
 
-def back_kernel(
-    info_ref, got_ref, residual_ref, mod_ref, w_out_ref, w_mel_ref, keep_ref, send_ref, attended,
-    after, speed,
-):
-    rows, width = residual_ref.shape
+def attend_first_kernel(info_ref, *refs):
+    chips = len(refs) - 4
+    got_refs = refs[:chips]
+    out_ref, keys, values, queries = refs[chips:]
+    gather_keys(info_ref, got_refs, keys, values)
+    attend_rows(got_refs[1::2], keys, values, out_ref, queries)
+
+
+def attend_second_kernel(info_ref, keys, values, *refs):
+    del info_ref
+    attend_rows(refs[:-2], keys, values, refs[-2], refs[-1])
+
+
+def merge_kernel(info_ref, own_ref, got_ref, *out_refs):
+    del info_ref
+    for at, out_ref in enumerate(out_refs):
+        out_ref[0] = own_ref[at + 1]
+        out_ref[1] = got_ref[at + 1]
+
+
+def back_kernel(blocks, info_ref, residual_hbm, w_mel_hbm, mod_ref, w_out_ref, *refs):
+    count = 1 + max(at for at, _, _ in blocks)
+    got_refs = refs[:count]
+    keep_ref, send_ref, attended, after, speed, residual, w_mel, sems = refs[count:]
+    rows, width = residual.shape
     tiles = width // LANES
-    core = info_ref[CORE]
-    for block in range(got_ref.shape[0]):
-        attended[:, block * LANES : (block + 1) * LANES] = got_ref[block]
+    core, chip = info_ref[CORE], info_ref[CHIP]
+    loads = [
+        pltpu.make_async_copy(residual_hbm, residual, sems.at[0]),
+        pltpu.make_async_copy(w_mel_hbm, w_mel, sems.at[1]),
+    ]
+    for load in loads:
+        load.start()
+    for at, place, apart in blocks:
+        group = place if apart is None else chip ^ apart
+        attended[:, tile_lanes(group)] = got_refs[at][place]
     wide = 2 * LANES
-    total = jnp.zeros((rows, LANES), jnp.float32)
     for block in range(width // wide):
         lanes = slice(block * wide, (block + 1) * wide)
         branch = jnp.dot(attended[...], w_out_ref[:, lanes], preferred_element_type=jnp.float32)
-        value = residual_ref[:, lanes] + mod_ref[2:3, lanes] * branch
+        after[:, lanes] = mod_ref[2:3, lanes] * branch
+    loads[0].wait()
+
+    def join(tile, total):
+        lanes = tile_lanes(tile)
+        value = residual[:, lanes] + after[:, lanes]
         after[:, lanes] = value
-        total = total + value[:, :LANES] + value[:, LANES:]
+        return total + value
+
+    total = lax.fori_loop(0, tiles, join, jnp.zeros((rows, LANES), jnp.float32), unroll=6)
 
     def store(lanes, value):
         after[:, lanes] = value
 
     row_norm(lambda tile: after[:, tile_lanes(tile)], store, tiles, mod_ref, 3, total)
+    loads[1].wait()
     speed[...] = lax.dot_general(
-        after[...].astype(jnp.bfloat16), w_mel_ref[...], (((1,), (1,)), ((), ())),
+        after[...].astype(jnp.bfloat16), w_mel[...], (((1,), (1,)), ((), ())),
         preferred_element_type=jnp.float32,
     )
     half = rows // 2
@@ -276,10 +298,9 @@
 def call(kernel, out_shape, inputs, scratch, limit, hbm=()):
     single = not isinstance(out_shape, tuple)
     specs = [hbm_spec() if at in hbm else vmem_spec() for at in range(1, len(inputs))]
-    inputs = [
-        pltpu.with_memory_space_constraint(value, pltpu.HBM) if at in hbm else value
-        for at, value in enumerate(inputs)
-    ]
+    inputs = list(inputs)
+    for at in hbm:
+        inputs[at] = pltpu.with_memory_space_constraint(inputs[at], pltpu.HBM)
     return pl.pallas_call(
         kernel,
         out_shape=out_shape,
@@ -406,22 +427,41 @@
         for side in range(2):
             apart = first + side
             held[apart] = across(made[side], 2 * apart, count) if apart else made[side]
-    total = chips * rows
-    attended = call(
-        attend_kernel,
-        array((chips, rows, LANES), jnp.bfloat16),
+    total, half = chips * rows, chips // 2
+    queries = VMEM((total, 2 * LANES), jnp.bfloat16)
+    crossing, keys, values = call(
+        attend_first_kernel,
+        (
+            array((half, rows, LANES), jnp.bfloat16),
+            array((total, 2 * LANES), jnp.bfloat16),
+            array((total, LANES), jnp.bfloat16),
+        ),
         (info,) + tuple(held[apart] for apart in range(chips)),
-        [
-            VMEM((total, 2 * LANES), jnp.bfloat16),
-            VMEM((total, LANES), jnp.bfloat16),
-            VMEM((2 * total, 2 * LANES), jnp.bfloat16),
-        ],
-        24,
-    )
-    return lax.all_to_all(
-        attended, "seq", split_axis=0, concat_axis=0, tiled=True,
-        axis_index_groups=same_core(count),
-    )
+        [queries],
+        16,
+    )
+    crossed = across(crossing, 2, count)
+    staying = call(
+        attend_second_kernel,
+        array((half, rows, LANES), jnp.bfloat16),
+        (info, keys, values) + tuple(held[apart] for apart in range(0, chips, 2)),
+        [queries],
+        16,
+    )
+    joined = call(
+        merge_kernel,
+        (array((2, rows, LANES), jnp.bfloat16),) * (half - 1),
+        (info, staying, crossed),
+        [],
+        4,
+    )
+    back, blocks = [staying, crossed], [(0, 0, 0), (1, 0, 1)]
+    apart_first = sorted(range(1, half), reverse=True)
+    got = {apart: across(joined[apart - 1], 4 * apart, count) for apart in apart_first}
+    for apart in range(1, half):
+        blocks += [(len(back), side, 2 * apart + side) for side in range(2)]
+        back.append(got[apart])
+    return back, blocks
 
 
 def per_device(
@@ -436,14 +476,9 @@
     place = jnp.stack([core, chip])
 
     partner = across(hidden, 1, count)
-    near, far = call(
-        edge_kernel,
-        (array((HALO, width), jnp.bfloat16),) * 2,
-        (place, hidden),
-        [pltpu.SemaphoreType.DMA((2,))],
-        4,
-        hbm=(1,),
-    )
+    edge = core * (rows - HALO)
+    near = lax.dynamic_slice(hidden, (1 - core, edge, 0), (1, HALO, width))[0]
+    far = lax.dynamic_slice(hidden, (core, edge, 0), (1, HALO, width))[0]
     steps = range(chips - 1)
     near = lax.ppermute(
         near, "seq",
@@ -480,28 +515,25 @@
         hbm=(7,),
     )
     if chips_hold_groups(count):
-        back = attend_chips(normed, weight, tables, info, count)
+        back, blocks = attend_chips(normed, weight, tables, info, count)
     else:
-        back = attend_any(normed, weight, tables, info, lengths[0], count)
+        back = [attend_any(normed, weight, tables, info, lengths[0], count)]
+        blocks = [(0, group, None) for group in range(back[0].shape[0])]
     mels = w_mel.shape[1]
-    residual, w_mel = call(
-        fetch_kernel,
-        (array(residual.shape), array((mels, width), jnp.bfloat16)),
-        (place, residual, w_mel.T),
-        [pltpu.SemaphoreType.DMA((2,))],
-        4,
-        hbm=(1, 2),
-    )
     keep, send = call(
-        back_kernel,
+        functools.partial(back_kernel, tuple(blocks)),
         (array((rows, mels)),) * 2,
-        (info, back, residual, mods, w_out, w_mel),
+        (info, residual, w_mel.T, mods, w_out) + tuple(back),
         [
             VMEM((chip_rows, HEADS * HEAD_DIM), jnp.bfloat16),
             VMEM((chip_rows, width), jnp.float32),
             VMEM((chip_rows, mels), jnp.float32),
+            VMEM((chip_rows, width), jnp.float32),
+            VMEM((mels, width), jnp.bfloat16),
+            pltpu.SemaphoreType.DMA((2,)),
         ],
         12,
+        hbm=(1, 2),
     )
     other = across(send, 1, count)
     first = jnp.where(core == 0, keep, other)

time: 63.2 us -> 64.8 us (1.025)
  waiting for transfers between devices: 14.3 us -> 16.8 us
  local copies, waits for them, and re-layouts: 3.67 us -> 1.44 us
  other arithmetic: 1.16 us -> 1.92 us
    ppermute x9 -> x13, waiting for transfers between devices: 5.86 us -> 13 us  [across(): return lax.ppermute(value, 'seq', [(i, i ^ apart) for i in range(count)])]
    ppermute x9 -> x13, starting transfers between devices: 14.2 us -> 19 us  [across(): return lax.ppermute(value, 'seq', [(i, i ^ apart) for i in range(count)])]
    all_to_all x1 -> x0, waiting for transfers between devices: 4.67 us -> none  [attend_chips(): lax.all_to_all(attended, 'seq', split_axis=0, concat_axis=0, tiled=True,...]
    all_to_all x1 -> x0, starting transfers between devices: 4.49 us -> none  [attend_chips(): lax.all_to_all(attended, 'seq', split_axis=0, concat_axis=0, tiled=True,...]
    unnamed x14 -> x6, local copies, waits for them, and re-layouts: 3.67 us -> 0.61 us
    squeeze x0 -> x1, local copies, waits for them, and re-layouts: none -> 0.83 us  [per_device(): far = lax.dynamic_slice(hidden, (core, edge, 0), (1, HALO, width))[0]]
    add x1, other arithmetic: 0.7 us -> 1.46 us  [per_device(): return (velocity, latent + (1.0 - time_now) * velocity)]
  transfers between devices with their start and end apart: 12 -> 15, of which waited for: 6 -> 8; matrix products, arithmetic and copies ran while one was open for 1% -> 2% of each run, Pallas kernels for 13% -> 12%
where the time goes in v1:
time: 64.8 us; the launch traced here: 64.4 us
  starting transfers between devices  20.9 us (32%)
  Pallas kernels  20.6 us (32%)
  waiting for transfers between devices  16.8 us (26%)
  between operations  2.82 us (4%)
  other arithmetic  1.92 us (3%)
  local copies, waits for them, and re-layouts  1.44 us (2%)
    pallas_call x10, Pallas kernels, call(): pl.pallas_call(kernel, out_shape=out_shape, in_specs=[smem_spec()] + spec...  20.6 us
    ppermute x13, starting transfers between devices, across(): return lax.ppermute(value, 'seq', [(i, i ^ apart) for i in range(count)])  19 us
    ppermute x13, waiting for transfers between devices, across(): return lax.ppermute(value, 'seq', [(i, i ^ apart) for i in range(count)])  13 us
    ppermute x1, waiting for transfers between devices, per_device(): lax.ppermute(far, 'seq', [(2 * m + 1, 2 * m + 3) for m in steps] + [(2 *...  3.73 us
    add x1, other arithmetic, per_device(): return (velocity, latent + (1.0 - time_now) * velocity)  1.46 us
  transfers between devices with their start and end apart: 15, of which 8 were waited for; matrix products, arithmetic and copies ran while one was open for 2% of the time, Pallas kernels for 12%

profile of v1, /device:TPU:0, one launch (start us, length us, event | category | flops | bytes accessed | tf_op | source)
XLA Modules:
  0.0 64.4 jit_solution(17615730055741379241)
XLA Ops:
  0.6 0.6 collective-permute-start
  1.2 0.8 %dynamic-slice_bitcast_fusion = (bf16[16,1536]{1,0:T(8,128)(2,1)S(1)}, bf16[16,1536]{1,0:T(8,128)(2,1)S(1)}) fusion(bf16[2,56,1536]{2,1,0:T(8,128)(2,1)} %hidden_hbm.1, s32[]{:T(128)S(6)} %select_n.56, s32[]{:T(128)S(6)} %select_n.55, s32[]{:T(128)S(6)} %select_n.54), kind=kLoop, calls=%fused_computation.3 | loop fusion | bytes 196620 | tf_op jit(solution)/shard_map/squeeze | solution.py:481
  2.0 0.7 %collective-permute-start.1 = (bf16[16,1536]{1,0:T(8,128)(2,1)S(1)}, bf16[16,1536]{1,0:T(8,128)(2,1)S(1)}, u32[]{:S(2)}, u32[]{:S(2)}) collective-permute-start(bf16[16,1536]{1,0:T(8,128)(2,1)S(1)} %get-tuple-element.49), channel_id=1, source_target_pairs={{1,2},{3,4},{5,6},{7,8},{9,10},{11,12},{13,14},{2,1},{4,3},{6,5},{... | collective-permute-start | bytes 147464 | tf_op jit(solution)/shard_map/ppermute | solution.py:483
  2.7 1.3 %collective-permute-start.2 = (bf16[16,1536]{1,0:T(8,128)(2,1)S(1)}, bf16[16,1536]{1,0:T(8,128)(2,1)S(1)}, u32[]{:S(2)}, u32[]{:S(2)}) collective-permute-start(bf16[16,1536]{1,0:T(8,128)(2,1)S(1)} %get-tuple-element.48), channel_id=1, source_target_pairs={{1,3},{3,5},{5,7},{7,9},{9,11},{11,13},{13,15},{2,0},{4,2},{6,4},{... | collective-permute-start | bytes 147464 | tf_op jit(solution)/shard_map/ppermute | solution.py:487
  4.0 0.1 pad_add_fusion.1.info_ref
  4.7 0.3 fusion
  5.0 0.1 pad_add_fusion.info_ref
  5.1 1.6 %shard_map.113 = (bf16[56,1536]{1,0:T(8,128)(2,1)S(1)}, f32[31,1536]{1,0:T(8,128)S(1)}, f32[5,1536]{1,0:T(8,128)S(1)}) custom-call(s32[2]{0:T(128)S(1)} %pad_add_fusion.1.info_ref, bf16[2,56,1536]{2,1,0:T(8,128)(2,1)} %hidden_hbm.1, f32[31,1536]{1,0:T(8,128)} %taps_hbm.1, f32[5,1536]{1,0:T(8,128)} %mod_hbm.1), custom_call_target="tpu_custom_call" | custom-call | tf_op jit(solution)/shard_map/pallas_call | solution.py:304
  6.7 0.0 collective-permute-done.1.near_ref
  6.7 3.7 %collective-permute-done.2.far_ref = bf16[16,1536]{1,0:T(8,128)(2,1)S(1)} collective-permute-done((bf16[16,1536]{1,0:T(8,128)(2,1)S(1)}, bf16[16,1536]{1,0:T(8,128)(2,1)S(1)}, u32[]{:S(2)}, u32[]{:S(2)}) %collective-permute-start.2) | collective-permute-done | bytes 49184 | tf_op jit(solution)/shard_map/ppermute | solution.py:487
  10.4 0.0 collective-permute-done.partner_ref
  10.4 4.3 %shard_map.114 = (f32[112,1536]{1,0:T(8,128)S(1)}, bf16[112,1536]{1,0:T(8,128)(2,1)S(1)}, bf16[1536,3072]{1,0:T(8,128)(2,1)S(1)}) custom-call(s32[3]{0:T(128)S(1)} %pad_add_fusion.info_ref, bf16[56,1536]{1,0:T(8,128)(2,1)S(1)} %get-tuple-element.24.own_ref, bf16[2,56,1536]{2,1,0:T(8,128)(2,1)S(1)} %collective-permute-done.partner_ref, ...), custom_call_target="tpu_custom_call" | custom-call | tf_op jit(solution)/shard_map/pallas_call | solution.py:304
  14.8 1.2 %shard_map.118 = (bf16[3,112,128]{2,1,0:T(8,128)(2,1)S(1)}, bf16[3,112,128]{2,1,0:T(8,128)(2,1)S(1)}) custom-call(s32[3]{0:T(128)S(1)} %pad_add_fusion.info_ref, bf16[112,1536]{1,0:T(8,128)(2,1)S(1)} %get-tuple-element.28.normed_ref, bf16[1536,3072]{1,0:T(8,128)(2,1)S(1)} %get-tuple-element.29.weight_ref, f32[112,128]{1,0:T(8,128)S(1)} %get-tuple-element.51.cos_ref, ...), custom_call_target="tpu_custom_call" | custom-call | tf_op jit(solution)/shard_map/pallas_call | solution.py:304
  15.9 6.2 %collective-permute-start.8 = (bf16[3,112,128]{2,1,0:T(8,128)(2,1)S(1)}, bf16[3,112,128]{2,1,0:T(8,128)(2,1)S(1)}, u32[]{:S(2)}, u32[]{:S(2)}) collective-permute-start(bf16[3,112,128]{2,1,0:T(8,128)(2,1)S(1)} %get-tuple-element.36), channel_id=1, source_target_pairs={{0,12},{1,13},{2,14},{3,15},{4,8},{5,9},{6,10},{7,11},{8,4},{9,5},... | collective-permute-start | bytes 258056 | tf_op jit(solution)/shard_map/ppermute | solution.py:334
  22.1 0.2 collective-permute-start.9
  22.4 1.2 %shard_map.117 = (bf16[3,112,128]{2,1,0:T(8,128)(2,1)S(1)}, bf16[3,112,128]{2,1,0:T(8,128)(2,1)S(1)}) custom-call(s32[3]{0:T(128)S(1)} %pad_add_fusion.info_ref, bf16[112,1536]{1,0:T(8,128)(2,1)S(1)} %get-tuple-element.28.normed_ref, bf16[1536,3072]{1,0:T(8,128)(2,1)S(1)} %get-tuple-element.29.weight_ref, f32[112,128]{1,0:T(8,128)S(1)} %get-tuple-element.51.cos_ref, ...), custom_call_target="tpu_custom_call" | custom-call | tf_op jit(solution)/shard_map/pallas_call | solution.py:304
  23.6 0.0 copy-start
  23.6 1.2 %shard_map.116 = (bf16[3,112,128]{2,1,0:T(8,128)(2,1)S(1)}, bf16[3,112,128]{2,1,0:T(8,128)(2,1)S(1)}) custom-call(s32[3]{0:T(128)S(1)} %pad_add_fusion.info_ref, bf16[112,1536]{1,0:T(8,128)(2,1)S(1)} %get-tuple-element.28.normed_ref, bf16[1536,3072]{1,0:T(8,128)(2,1)S(1)} %get-tuple-element.29.weight_ref, f32[112,128]{1,0:T(8,128)S(1)} %get-tuple-element.51.cos_ref, ...), custom_call_target="tpu_custom_call" | custom-call | tf_op jit(solution)/shard_map/pallas_call | solution.py:304
  24.8 1.2 %shard_map.115 = (bf16[3,112,128]{2,1,0:T(8,128)(2,1)S(1)}, bf16[3,112,128]{2,1,0:T(8,128)(2,1)S(1)}) custom-call(s32[3]{0:T(128)S(1)} %pad_add_fusion.info_ref, bf16[112,1536]{1,0:T(8,128)(2,1)S(1)} %get-tuple-element.28.normed_ref, bf16[1536,3072]{1,0:T(8,128)(2,1)S(1)} %get-tuple-element.29.weight_ref, f32[112,128]{1,0:T(8,128)S(1)} %get-tuple-element.51.cos_ref, ...), custom_call_target="tpu_custom_call" | custom-call | tf_op jit(solution)/shard_map/pallas_call | solution.py:304
  26.0 1.2 %collective-permute-start.6 = (bf16[3,112,128]{2,1,0:T(8,128)(2,1)S(1)}, bf16[3,112,128]{2,1,0:T(8,128)(2,1)S(1)}, u32[]{:S(2)}, u32[]{:S(2)}) collective-permute-start(bf16[3,112,128]{2,1,0:T(8,128)(2,1)S(1)} %get-tuple-element.34), channel_id=1, source_target_pairs={{0,8},{1,9},{2,10},{3,11},{4,12},{5,13},{6,14},{7,15},{8,0},{9,1},... | collective-permute-start | bytes 258056 | tf_op jit(solution)/shard_map/ppermute | solution.py:334
  27.2 2.5 %collective-permute-start.7 = (bf16[3,112,128]{2,1,0:T(8,128)(2,1)S(1)}, bf16[3,112,128]{2,1,0:T(8,128)(2,1)S(1)}, u32[]{:S(2)}, u32[]{:S(2)}) collective-permute-start(bf16[3,112,128]{2,1,0:T(8,128)(2,1)S(1)} %get-tuple-element.35), channel_id=1, source_target_pairs={{0,10},{1,11},{2,8},{3,9},{4,14},{5,15},{6,12},{7,13},{8,2},{9,3},... | collective-permute-start | bytes 258056 | tf_op jit(solution)/shard_map/ppermute | solution.py:334
  29.7 1.4 %collective-permute-start.4 = (bf16[3,112,128]{2,1,0:T(8,128)(2,1)S(1)}, bf16[3,112,128]{2,1,0:T(8,128)(2,1)S(1)}, u32[]{:S(2)}, u32[]{:S(2)}) collective-permute-start(bf16[3,112,128]{2,1,0:T(8,128)(2,1)S(1)} %get-tuple-element.32), channel_id=1, source_target_pairs={{0,4},{1,5},{2,6},{3,7},{4,0},{5,1},{6,2},{7,3},{8,12},{9,13},{10,... | collective-permute-start | bytes 258056 | tf_op jit(solution)/shard_map/ppermute | solution.py:334
  31.1 0.0 collective-permute-done.8.refs_6_.refs_3_
  31.1 0.8 %collective-permute-start.5 = (bf16[3,112,128]{2,1,0:T(8,128)(2,1)S(1)}, bf16[3,112,128]{2,1,0:T(8,128)(2,1)S(1)}, u32[]{:S(2)}, u32[]{:S(2)}) collective-permute-start(bf16[3,112,128]{2,1,0:T(8,128)(2,1)S(1)} %get-tuple-element.33), channel_id=1, source_target_pairs={{0,6},{1,7},{2,4},{3,5},{4,2},{5,3},{6,0},{7,1},{8,14},{9,15},{10,... | collective-permute-start | bytes 258056 | tf_op jit(solution)/shard_map/ppermute | solution.py:334
  31.9 0.0 collective-permute-done.9.refs_7_
  31.9 1.3 %collective-permute-start.3 = (bf16[3,112,128]{2,1,0:T(8,128)(2,1)S(1)}, bf16[3,112,128]{2,1,0:T(8,128)(2,1)S(1)}, u32[]{:S(2)}, u32[]{:S(2)}) collective-permute-start(bf16[3,112,128]{2,1,0:T(8,128)(2,1)S(1)} %get-tuple-element.31), channel_id=1, source_target_pairs={{0,2},{1,3},{2,0},{3,1},{4,6},{5,7},{6,4},{7,5},{8,10},{9,11},{10,... | collective-permute-start | bytes 258056 | tf_op jit(solution)/shard_map/ppermute | solution.py:334
  33.2 1.1 %collective-permute-done.6.refs_4_.refs_2_ = bf16[3,112,128]{2,1,0:T(8,128)(2,1)S(1)} collective-permute-done((bf16[3,112,128]{2,1,0:T(8,128)(2,1)S(1)}, bf16[3,112,128]{2,1,0:T(8,128)(2,1)S(1)}, u32[]{:S(2)}, u32[]{:S(2)}) %collective-permute-start.6) | collective-permute-done | bytes 86048 | tf_op jit(solution)/shard_map/ppermute | solution.py:334
  34.3 3.1 %collective-permute-done.7.refs_5_ = bf16[3,112,128]{2,1,0:T(8,128)(2,1)S(1)} collective-permute-done((bf16[3,112,128]{2,1,0:T(8,128)(2,1)S(1)}, bf16[3,112,128]{2,1,0:T(8,128)(2,1)S(1)}, u32[]{:S(2)}, u32[]{:S(2)}) %collective-permute-start.7) | collective-permute-done | bytes 86048 | tf_op jit(solution)/shard_map/ppermute | solution.py:334
  37.4 0.0 collective-permute-done.4.refs_2_.refs_1_
  37.4 1.4 %collective-permute-done.5.refs_3_ = bf16[3,112,128]{2,1,0:T(8,128)(2,1)S(1)} collective-permute-done((bf16[3,112,128]{2,1,0:T(8,128)(2,1)S(1)}, bf16[3,112,128]{2,1,0:T(8,128)(2,1)S(1)}, u32[]{:S(2)}, u32[]{:S(2)}) %collective-permute-start.5) | collective-permute-done | bytes 86048 | tf_op jit(solution)/shard_map/ppermute | solution.py:334
  38.8 0.3 collective-permute-done.3.refs_1_
  39.1 2.4 %shard_map.119 = (bf16[4,112,128]{2,1,0:T(8,128)(2,1)S(1)}, bf16[896,256]{1,0:T(8,128)(2,1)S(1)}, bf16[896,128]{1,0:T(8,128)(2,1)S(1)}) custom-call(s32[3]{0:T(128)S(1)} %pad_add_fusion.info_ref, bf16[3,112,128]{2,1,0:T(8,128)(2,1)S(1)} %get-tuple-element.30.refs_0_, bf16[3,112,128]{2,1,0:T(8,128)(2,1)S(1)} %collective-permute-done.3.refs_1_, ...), custom_call_target="tpu_custom_call" | custom-call | tf_op jit(solution)/shard_map/pallas_call | solution.py:304
  41.4 0.4 collective-permute-start.10
  41.8 2.3 %shard_map.120.own_ref.refs_0_ = bf16[4,112,128]{2,1,0:T(8,128)(2,1)S(1)} custom-call(s32[3]{0:T(128)S(1)} %pad_add_fusion.info_ref, bf16[896,256]{1,0:T(8,128)(2,1)S(1)} %get-tuple-element.38.keys, bf16[896,128]{1,0:T(8,128)(2,1)S(1)} %get-tuple-element.39.values, bf16[3,112,128]{2,1,0:T(8,128)(2,1)S(1)} %get-tuple-element.30.refs_0_, ...), custom_call_target="tpu_custom_call" | custom-call | tf_op jit(solution)/shard_map/pallas_call | solution.py:304
  44.1 2.2 %collective-permute-done.10.got_ref.refs_1_ = bf16[4,112,128]{2,1,0:T(8,128)(2,1)S(1)} collective-permute-done((bf16[4,112,128]{2,1,0:T(8,128)(2,1)S(1)}, bf16[4,112,128]{2,1,0:T(8,128)(2,1)S(1)}, u32[]{:S(2)}, u32[]{:S(2)}) %collective-permute-start.10) | collective-permute-done | bytes 114720 | tf_op jit(solution)/shard_map/ppermute | solution.py:334
  46.3 1.2 %shard_map.121 = (bf16[2,112,128]{2,1,0:T(8,128)(2,1)}, bf16[2,112,128]{2,1,0:T(8,128)(2,1)}, bf16[2,112,128]{2,1,0:T(8,128)(2,1)}) custom-call(s32[3]{0:T(128)S(1)} %pad_add_fusion.info_ref, bf16[4,112,128]{2,1,0:T(8,128)(2,1)S(1)} %shard_map.120.own_ref.refs_0_, bf16[4,112,128]{2,1,0:T(8,128)(2,1)S(1)} %collective-permute-done.10.got_ref.refs_1_), custom_call_target="tpu_custom_call" | custom-call | tf_op jit(solution)/shard_map/pallas_call | solution.py:304
  47.5 0.0 collective-permute-start.11
  47.5 3.0 %collective-permute-start.12 = (bf16[2,112,128]{2,1,0:T(8,128)(2,1)}, bf16[2,112,128]{2,1,0:T(8,128)(2,1)S(1)}, u32[]{:S(2)}, u32[]{:S(2)}) collective-permute-start(bf16[2,112,128]{2,1,0:T(8,128)(2,1)} %get-tuple-element.42), channel_id=1, source_target_pairs={{0,8},{1,9},{2,10},{3,11},{4,12},{5,13},{6,14},{7,15},{8,0},{9,1},... | collective-permute-start | bytes 172040 | tf_op jit(solution)/shard_map/ppermute | solution.py:334
  50.5 1.4 %collective-permute-start.13 = (bf16[2,112,128]{2,1,0:T(8,128)(2,1)}, bf16[2,112,128]{2,1,0:T(8,128)(2,1)}, u32[]{:S(2)}, u32[]{:S(2)}) collective-permute-start(bf16[2,112,128]{2,1,0:T(8,128)(2,1)} %get-tuple-element.43), channel_id=1, source_target_pairs={{0,12},{1,13},{2,14},{3,15},{4,8},{5,9},{6,10},{7,11},{8,4},{9,5},... | collective-permute-start | bytes 172040 | tf_op jit(solution)/shard_map/ppermute | solution.py:334
  51.9 1.2 %collective-permute-done.11.refs_2_ = bf16[2,112,128]{2,1,0:T(8,128)(2,1)S(1)} collective-permute-done((bf16[2,112,128]{2,1,0:T(8,128)(2,1)}, bf16[2,112,128]{2,1,0:T(8,128)(2,1)S(1)}, u32[]{:S(2)}, u32[]{:S(2)}) %collective-permute-start.11) | collective-permute-done | bytes 57376 | tf_op jit(solution)/shard_map/ppermute | solution.py:334
  53.1 0.0 collective-permute-done.12.refs_3_
  53.1 3.7 %collective-permute-done.13.refs_4_ = bf16[2,112,128]{2,1,0:T(8,128)(2,1)} collective-permute-done((bf16[2,112,128]{2,1,0:T(8,128)(2,1)}, bf16[2,112,128]{2,1,0:T(8,128)(2,1)}, u32[]{:S(2)}, u32[]{:S(2)}) %collective-permute-start.13) | collective-permute-done | bytes 57376 | tf_op jit(solution)/shard_map/ppermute | solution.py:334
  56.8 4.1 %shard_map.122 = (f32[56,100]{1,0:T(8,128)S(1)}, f32[56,100]{1,0:T(8,128)}) custom-call(s32[3]{0:T(128)S(1)} %pad_add_fusion.info_ref, f32[112,1536]{1,0:T(8,128)} %copy-done.1, bf16[100,1536]{1,0:T(8,128)(2,1)} %bitcast.12, f32[5,1536]{1,0:T(8,128)S(1)} %get-tuple-element.26.mod_ref, bf16[1024,1536]{1,0:T(8,128)(2,1)S(1)} %copy-done, ...), custom_call_target="tpu_custom_call" | custom-call | tf_op jit(solution)/shard_map/pallas_call | solution.py:304
  60.9 0.0 copy-start.2
  60.9 0.6 copy-done.2
  61.5 0.0 collective-permute-start.14
  62.9 0.0 collective-permute-done.14
  62.9 1.5 %multiply_add_fusion = (f32[56,100]{1,0:T(8,128)}, f32[56,100]{1,0:T(8,128)}) fusion(f32[56,100]{1,0:T(8,128)} %param.11, f32[]{:T(128)} %bitcast.7, f32[56,100]{1,0:T(8,128)S(1)} %collective-permute-done.14, f32[56,100]{1,0:T(8,128)} %copy-done.2, f32[]{:T(128)} %bitcast.11, pred[]{:T(512)S(6)} %eq.7, pred[56]{0:T(512)(128)(4,1)S(1)} %add_compare_fusion), kind=kLoop, calls=%fused_computation.5 | loop fusion | flops 44800 | bytes 112065 | tf_op jit(solution)/shard_map/add | solution.py:546
  (6 shorter events, 0.0 us)
Async XLA Ops:
  0.6 9.8 %collective-permute-start = (bf16[2,56,1536]{2,1,0:T(8,128)(2,1)}, bf16[2,56,1536]{2,1,0:T(8,128)(2,1)S(1)}, u32[]{:S(2)}, u32[]{:S(2)}) collective-permute-start(bf16[2,56,1536]{2,1,0:T(8,128)(2,1)} %hidden_hbm.1), channel_id=1, source_target_pairs={{0,1},{1,0},{2,3},{3,2},{4,5},{5,4},{6,7},{7,6},{8,9},{9,8},{10,11... | collective-permute-start | bytes 1032200 | tf_op jit(solution)/shard_map/ppermute | solution.py:334
  2.0 4.7 %collective-permute-start.1 = (bf16[16,1536]{1,0:T(8,128)(2,1)S(1)}, bf16[16,1536]{1,0:T(8,128)(2,1)S(1)}, u32[]{:S(2)}, u32[]{:S(2)}) collective-permute-start(bf16[16,1536]{1,0:T(8,128)(2,1)S(1)} %get-tuple-element.49), channel_id=1, source_target_pairs={{1,2},{3,4},{5,6},{7,8},{9,10},{11,12},{13,14},{2,1},{4,3},{6,5},{... | collective-permute-start | bytes 147464 | tf_op jit(solution)/shard_map/ppermute | solution.py:483
  2.7 7.8 %collective-permute-start.2 = (bf16[16,1536]{1,0:T(8,128)(2,1)S(1)}, bf16[16,1536]{1,0:T(8,128)(2,1)S(1)}, u32[]{:S(2)}, u32[]{:S(2)}) collective-permute-start(bf16[16,1536]{1,0:T(8,128)(2,1)S(1)} %get-tuple-element.48), channel_id=1, source_target_pairs={{1,3},{3,5},{5,7},{7,9},{9,11},{11,13},{13,15},{2,0},{4,2},{6,4},{... | collective-permute-start | bytes 147464 | tf_op jit(solution)/shard_map/ppermute | solution.py:487
  14.8 8.8 %copy-start.1 = (f32[112,1536]{1,0:T(8,128)}, f32[112,1536]{1,0:T(8,128)S(1)}, u32[]{:S(2)}) copy-start(f32[112,1536]{1,0:T(8,128)S(1)} %get-tuple-element.27.residual_hbm) | copy-start | bytes 2064388
  15.9 15.2 %collective-permute-start.8 = (bf16[3,112,128]{2,1,0:T(8,128)(2,1)S(1)}, bf16[3,112,128]{2,1,0:T(8,128)(2,1)S(1)}, u32[]{:S(2)}, u32[]{:S(2)}) collective-permute-start(bf16[3,112,128]{2,1,0:T(8,128)(2,1)S(1)} %get-tuple-element.36), channel_id=1, source_target_pairs={{0,12},{1,13},{2,14},{3,15},{4,8},{5,9},{6,10},{7,11},{8,4},{9,5},... | collective-permute-start | bytes 258056 | tf_op jit(solution)/shard_map/ppermute | solution.py:334
  22.1 9.8 %collective-permute-start.9 = (bf16[3,112,128]{2,1,0:T(8,128)(2,1)S(1)}, bf16[3,112,128]{2,1,0:T(8,128)(2,1)S(1)}, u32[]{:S(2)}, u32[]{:S(2)}) collective-permute-start(bf16[3,112,128]{2,1,0:T(8,128)(2,1)S(1)} %get-tuple-element.37), channel_id=1, source_target_pairs={{0,14},{1,15},{2,12},{3,13},{4,10},{5,11},{6,8},{7,9},{8,6},{9,7},... | collective-permute-start | bytes 258056 | tf_op jit(solution)/shard_map/ppermute | solution.py:334
  23.6 33.2 %copy-start = (bf16[1024,1536]{1,0:T(8,128)(2,1)S(1)}, bf16[1024,1536]{1,0:T(8,128)(2,1)}, u32[]{:S(2)}) copy-start(bf16[1024,1536]{1,0:T(8,128)(2,1)} %w_out_ref.1) | copy-start | bytes 9437188
  26.0 8.3 %collective-permute-start.6 = (bf16[3,112,128]{2,1,0:T(8,128)(2,1)S(1)}, bf16[3,112,128]{2,1,0:T(8,128)(2,1)S(1)}, u32[]{:S(2)}, u32[]{:S(2)}) collective-permute-start(bf16[3,112,128]{2,1,0:T(8,128)(2,1)S(1)} %get-tuple-element.34), channel_id=1, source_target_pairs={{0,8},{1,9},{2,10},{3,11},{4,12},{5,13},{6,14},{7,15},{8,0},{9,1},... | collective-permute-start | bytes 258056 | tf_op jit(solution)/shard_map/ppermute | solution.py:334
  27.2 10.2 %collective-permute-start.7 = (bf16[3,112,128]{2,1,0:T(8,128)(2,1)S(1)}, bf16[3,112,128]{2,1,0:T(8,128)(2,1)S(1)}, u32[]{:S(2)}, u32[]{:S(2)}) collective-permute-start(bf16[3,112,128]{2,1,0:T(8,128)(2,1)S(1)} %get-tuple-element.35), channel_id=1, source_target_pairs={{0,10},{1,11},{2,8},{3,9},{4,14},{5,15},{6,12},{7,13},{8,2},{9,3},... | collective-permute-start | bytes 258056 | tf_op jit(solution)/shard_map/ppermute | solution.py:334
  29.7 7.7 %collective-permute-start.4 = (bf16[3,112,128]{2,1,0:T(8,128)(2,1)S(1)}, bf16[3,112,128]{2,1,0:T(8,128)(2,1)S(1)}, u32[]{:S(2)}, u32[]{:S(2)}) collective-permute-start(bf16[3,112,128]{2,1,0:T(8,128)(2,1)S(1)} %get-tuple-element.32), channel_id=1, source_target_pairs={{0,4},{1,5},{2,6},{3,7},{4,0},{5,1},{6,2},{7,3},{8,12},{9,13},{10,... | collective-permute-start | bytes 258056 | tf_op jit(solution)/shard_map/ppermute | solution.py:334
  31.1 7.7 %collective-permute-start.5 = (bf16[3,112,128]{2,1,0:T(8,128)(2,1)S(1)}, bf16[3,112,128]{2,1,0:T(8,128)(2,1)S(1)}, u32[]{:S(2)}, u32[]{:S(2)}) collective-permute-start(bf16[3,112,128]{2,1,0:T(8,128)(2,1)S(1)} %get-tuple-element.33), channel_id=1, source_target_pairs={{0,6},{1,7},{2,4},{3,5},{4,2},{5,3},{6,0},{7,1},{8,14},{9,15},{10,... | collective-permute-start | bytes 258056 | tf_op jit(solution)/shard_map/ppermute | solution.py:334
  31.9 7.1 %collective-permute-start.3 = (bf16[3,112,128]{2,1,0:T(8,128)(2,1)S(1)}, bf16[3,112,128]{2,1,0:T(8,128)(2,1)S(1)}, u32[]{:S(2)}, u32[]{:S(2)}) collective-permute-start(bf16[3,112,128]{2,1,0:T(8,128)(2,1)S(1)} %get-tuple-element.31), channel_id=1, source_target_pairs={{0,2},{1,3},{2,0},{3,1},{4,6},{5,7},{6,4},{7,5},{8,10},{9,11},{10,... | collective-permute-start | bytes 258056 | tf_op jit(solution)/shard_map/ppermute | solution.py:334
  41.4 4.9 %collective-permute-start.10 = (bf16[4,112,128]{2,1,0:T(8,128)(2,1)S(1)}, bf16[4,112,128]{2,1,0:T(8,128)(2,1)S(1)}, u32[]{:S(2)}, u32[]{:S(2)}) collective-permute-start(bf16[4,112,128]{2,1,0:T(8,128)(2,1)S(1)} %get-tuple-element.40), channel_id=1, source_target_pairs={{0,2},{1,3},{2,0},{3,1},{4,6},{5,7},{6,4},{7,5},{8,10},{9,11},{10,... | collective-permute-start | bytes 344072 | tf_op jit(solution)/shard_map/ppermute | solution.py:334
  47.5 5.6 %collective-permute-start.11 = (bf16[2,112,128]{2,1,0:T(8,128)(2,1)}, bf16[2,112,128]{2,1,0:T(8,128)(2,1)S(1)}, u32[]{:S(2)}, u32[]{:S(2)}) collective-permute-start(bf16[2,112,128]{2,1,0:T(8,128)(2,1)} %get-tuple-element.41), channel_id=1, source_target_pairs={{0,4},{1,5},{2,6},{3,7},{4,0},{5,1},{6,2},{7,3},{8,12},{9,13},{10,... | collective-permute-start | bytes 172040 | tf_op jit(solution)/shard_map/ppermute | solution.py:334
  47.5 5.6 %collective-permute-start.12 = (bf16[2,112,128]{2,1,0:T(8,128)(2,1)}, bf16[2,112,128]{2,1,0:T(8,128)(2,1)S(1)}, u32[]{:S(2)}, u32[]{:S(2)}) collective-permute-start(bf16[2,112,128]{2,1,0:T(8,128)(2,1)} %get-tuple-element.42), channel_id=1, source_target_pairs={{0,8},{1,9},{2,10},{3,11},{4,12},{5,13},{6,14},{7,15},{8,0},{9,1},... | collective-permute-start | bytes 172040 | tf_op jit(solution)/shard_map/ppermute | solution.py:334
  50.5 6.3 %collective-permute-start.13 = (bf16[2,112,128]{2,1,0:T(8,128)(2,1)}, bf16[2,112,128]{2,1,0:T(8,128)(2,1)}, u32[]{:S(2)}, u32[]{:S(2)}) collective-permute-start(bf16[2,112,128]{2,1,0:T(8,128)(2,1)} %get-tuple-element.43), channel_id=1, source_target_pairs={{0,12},{1,13},{2,14},{3,15},{4,8},{5,9},{6,10},{7,11},{8,4},{9,5},... | collective-permute-start | bytes 172040 | tf_op jit(solution)/shard_map/ppermute | solution.py:334
  60.9 0.6 copy-start.2
  61.5 1.4 %collective-permute-start.14 = (f32[56,100]{1,0:T(8,128)}, f32[56,100]{1,0:T(8,128)S(1)}, u32[]{:S(2)}, u32[]{:S(2)}) collective-permute-start(f32[56,100]{1,0:T(8,128)} %get-tuple-element.45), channel_id=1, source_target_pairs={{0,1},{1,0},{2,3},{3,2},{4,5},{5,4},{6,7},{7,6},{8,9},{9,8},{10,11... | collective-permute-start | bytes 67208 | tf_op jit(solution)/shard_map/ppermute | solution.py:334

commit v2 on v1

--- a/solution.py
+++ b/solution.py
@@ -199,7 +199,7 @@
         values[here, :] = got_ref[2]
 
 
-def attend_rows(query_refs, keys, values, out_ref, queries):
+def attend_rows(query_refs, keys, values, out_ref, queries, chip):
     _, rows, _ = query_refs[0].shape
     low = lax.broadcasted_iota(jnp.int32, (rows, LANES), 1) < HEAD_DIM
     zero = jnp.zeros((rows, LANES), jnp.bfloat16)
@@ -225,47 +225,34 @@
         mixed = mixed / weight_sum
         for side in range(2):
             base = 2 * side * rows
-            out_ref[first + side] = jnp.where(
+            out_ref[chip ^ (first + side)] = jnp.where(
                 low, mixed[base : base + rows], mixed[base + rows : base + 2 * rows]
             ).astype(jnp.bfloat16)
 
 
-def attend_first_kernel(info_ref, *refs):
+def attend_kernel(info_ref, *refs):
     chips = len(refs) - 4
     got_refs = refs[:chips]
     out_ref, keys, values, queries = refs[chips:]
     gather_keys(info_ref, got_refs, keys, values)
-    attend_rows(got_refs[1::2], keys, values, out_ref, queries)
-
-
-def attend_second_kernel(info_ref, keys, values, *refs):
-    del info_ref
-    attend_rows(refs[:-2], keys, values, refs[-2], refs[-1])
-
-
-def merge_kernel(info_ref, own_ref, got_ref, *out_refs):
-    del info_ref
-    for at, out_ref in enumerate(out_refs):
-        out_ref[0] = own_ref[at + 1]
-        out_ref[1] = got_ref[at + 1]
-
-
-def back_kernel(blocks, info_ref, residual_hbm, w_mel_hbm, mod_ref, w_out_ref, *refs):
-    count = 1 + max(at for at, _, _ in blocks)
-    got_refs = refs[:count]
-    keep_ref, send_ref, attended, after, speed, residual, w_mel, sems = refs[count:]
+    attend_rows(got_refs, keys, values, out_ref, queries, info_ref[CHIP])
+
+
+def back_kernel(
+    info_ref, residual_hbm, w_mel_hbm, mod_ref, w_out_ref, got_ref, keep_ref, send_ref, attended,
+    after, speed, residual, w_mel, sems,
+):
     rows, width = residual.shape
     tiles = width // LANES
-    core, chip = info_ref[CORE], info_ref[CHIP]
+    core = info_ref[CORE]
     loads = [
         pltpu.make_async_copy(residual_hbm, residual, sems.at[0]),
         pltpu.make_async_copy(w_mel_hbm, w_mel, sems.at[1]),
     ]
     for load in loads:
         load.start()
-    for at, place, apart in blocks:
-        group = place if apart is None else chip ^ apart
-        attended[:, tile_lanes(group)] = got_refs[at][place]
+    for group in range(got_ref.shape[0]):
+        attended[:, group * LANES : (group + 1) * LANES] = got_ref[group]
     wide = 2 * LANES
     for block in range(width // wide):
         lanes = slice(block * wide, (block + 1) * wide)
@@ -427,41 +414,22 @@
         for side in range(2):
             apart = first + side
             held[apart] = across(made[side], 2 * apart, count) if apart else made[side]
-    total, half = chips * rows, chips // 2
-    queries = VMEM((total, 2 * LANES), jnp.bfloat16)
-    crossing, keys, values = call(
-        attend_first_kernel,
-        (
-            array((half, rows, LANES), jnp.bfloat16),
-            array((total, 2 * LANES), jnp.bfloat16),
-            array((total, LANES), jnp.bfloat16),
-        ),
+    total = chips * rows
+    attended = call(
+        attend_kernel,
+        array((chips, rows, LANES), jnp.bfloat16),
         (info,) + tuple(held[apart] for apart in range(chips)),
-        [queries],
-        16,
-    )
-    crossed = across(crossing, 2, count)
-    staying = call(
-        attend_second_kernel,
-        array((half, rows, LANES), jnp.bfloat16),
-        (info, keys, values) + tuple(held[apart] for apart in range(0, chips, 2)),
-        [queries],
-        16,
-    )
-    joined = call(
-        merge_kernel,
-        (array((2, rows, LANES), jnp.bfloat16),) * (half - 1),
-        (info, staying, crossed),
-        [],
-        4,
-    )
-    back, blocks = [staying, crossed], [(0, 0, 0), (1, 0, 1)]
-    apart_first = sorted(range(1, half), reverse=True)
-    got = {apart: across(joined[apart - 1], 4 * apart, count) for apart in apart_first}
-    for apart in range(1, half):
-        blocks += [(len(back), side, 2 * apart + side) for side in range(2)]
-        back.append(got[apart])
-    return back, blocks
+        [
+            VMEM((total, 2 * LANES), jnp.bfloat16),
+            VMEM((total, LANES), jnp.bfloat16),
+            VMEM((2 * total, 2 * LANES), jnp.bfloat16),
+        ],
+        24,
+    )
+    return lax.all_to_all(
+        attended, "seq", split_axis=0, concat_axis=0, tiled=True,
+        axis_index_groups=same_core(count),
+    )
 
 
 def per_device(
@@ -515,15 +483,14 @@
         hbm=(7,),
     )
     if chips_hold_groups(count):
-        back, blocks = attend_chips(normed, weight, tables, info, count)
+        back = attend_chips(normed, weight, tables, info, count)
     else:
-        back = [attend_any(normed, weight, tables, info, lengths[0], count)]
-        blocks = [(0, group, None) for group in range(back[0].shape[0])]
+        back = attend_any(normed, weight, tables, info, lengths[0], count)
     mels = w_mel.shape[1]
     keep, send = call(
-        functools.partial(back_kernel, tuple(blocks)),
+        back_kernel,
         (array((rows, mels)),) * 2,
-        (info, residual, w_mel.T, mods, w_out) + tuple(back),
+        (info, residual, w_mel.T, mods, w_out, back),
         [
             VMEM((chip_rows, HEADS * HEAD_DIM), jnp.bfloat16),
             VMEM((chip_rows, width), jnp.float32),

time: 64.8 us -> 61.5 us (0.949)
  Pallas kernels: 20.6 us -> 18.1 us
  waiting for transfers between devices: 16.8 us -> 17.6 us
  other arithmetic: 1.92 us -> 1.16 us
    all_to_all x0 -> x1, waiting for transfers between devices: none -> 8 us  [attend_chips(): lax.all_to_all(attended, 'seq', split_axis=0, concat_axis=0, tiled=True,...]
    ppermute x13 -> x9, waiting for transfers between devices: 13 us -> 5.88 us  [across(): return lax.ppermute(value, 'seq', [(i, i ^ apart) for i in range(count)])]
    ppermute x13 -> x9, starting transfers between devices: 19 us -> 14.2 us  [across(): return lax.ppermute(value, 'seq', [(i, i ^ apart) for i in range(count)])]
    all_to_all x0 -> x1, starting transfers between devices: none -> 4.45 us  [attend_chips(): lax.all_to_all(attended, 'seq', split_axis=0, concat_axis=0, tiled=True,...]
    pallas_call x10 -> x8, Pallas kernels: 20.6 us -> 18.1 us  [call(): pl.pallas_call(kernel, out_shape=out_shape, in_specs=[smem_spec()] + spec...]
    add x1, other arithmetic: 1.46 us -> 0.7 us  [per_device(): return (velocity, latent + (1.0 - time_now) * velocity)]
  transfers between devices with their start and end apart: 15 -> 12, of which waited for: 8 -> 6; matrix products, arithmetic and copies ran while one was open for 2% -> 2% of each run, Pallas kernels for 12% -> 8%
where the time goes in v2:
time: 61.5 us; the launch traced here: 61.1 us
  starting transfers between devices  20.6 us (33%)
  Pallas kernels  18.1 us (29%)
  waiting for transfers between devices  17.6 us (29%)
  between operations  2.83 us (5%)
  other arithmetic  1.16 us (2%)
  local copies, waits for them, and re-layouts  0.85 us (1%)
    pallas_call x8, Pallas kernels, call(): pl.pallas_call(kernel, out_shape=out_shape, in_specs=[smem_spec()] + spec...  18.1 us
    ppermute x9, starting transfers between devices, across(): return lax.ppermute(value, 'seq', [(i, i ^ apart) for i in range(count)])  14.2 us
    all_to_all x1, waiting for transfers between devices, attend_chips(): lax.all_to_all(attended, 'seq', split_axis=0, concat_axis=0, tiled=True,...  8 us
    ppermute x9, waiting for transfers between devices, across(): return lax.ppermute(value, 'seq', [(i, i ^ apart) for i in range(count)])  5.88 us
    all_to_all x1, starting transfers between devices, attend_chips(): lax.all_to_all(attended, 'seq', split_axis=0, concat_axis=0, tiled=True,...  4.45 us
    ppermute x1, waiting for transfers between devices, per_device(): lax.ppermute(far, 'seq', [(2 * m + 1, 2 * m + 3) for m in steps] + [(2 *...  3.73 us
    ppermute x1, starting transfers between devices, per_device(): lax.ppermute(far, 'seq', [(2 * m + 1, 2 * m + 3) for m in steps] + [(2 *...  1.29 us
  transfers between devices with their start and end apart: 12, of which 6 were waited for; matrix products, arithmetic and copies ran while one was open for 2% of the time, Pallas kernels for 8%

profile of v2, /device:TPU:0, one launch (start us, length us, event | category | flops | bytes accessed | tf_op | source)
XLA Modules:
  0.0 61.1 jit_solution(2087355058516574442)
XLA Ops:
  0.6 0.6 collective-permute-start
  1.2 0.8 %dynamic-slice_bitcast_fusion = (bf16[16,1536]{1,0:T(8,128)(2,1)S(1)}, bf16[16,1536]{1,0:T(8,128)(2,1)S(1)}) fusion(bf16[2,56,1536]{2,1,0:T(8,128)(2,1)} %hidden_hbm.1, s32[]{:T(128)S(6)} %select_n.56, s32[]{:T(128)S(6)} %select_n.55, s32[]{:T(128)S(6)} %select_n.54), kind=kLoop, calls=%fused_computation.3 | loop fusion | bytes 196620 | tf_op jit(solution)/shard_map/squeeze | solution.py:449
  2.0 0.7 %collective-permute-start.1 = (bf16[16,1536]{1,0:T(8,128)(2,1)S(1)}, bf16[16,1536]{1,0:T(8,128)(2,1)S(1)}, u32[]{:S(2)}, u32[]{:S(2)}) collective-permute-start(bf16[16,1536]{1,0:T(8,128)(2,1)S(1)} %get-tuple-element.37), channel_id=1, source_target_pairs={{1,2},{3,4},{5,6},{7,8},{9,10},{11,12},{13,14},{2,1},{4,3},{6,5},{... | collective-permute-start | bytes 147464 | tf_op jit(solution)/shard_map/ppermute | solution.py:451
  2.7 1.3 %collective-permute-start.2 = (bf16[16,1536]{1,0:T(8,128)(2,1)S(1)}, bf16[16,1536]{1,0:T(8,128)(2,1)S(1)}, u32[]{:S(2)}, u32[]{:S(2)}) collective-permute-start(bf16[16,1536]{1,0:T(8,128)(2,1)S(1)} %get-tuple-element.36), channel_id=1, source_target_pairs={{1,3},{3,5},{5,7},{7,9},{9,11},{11,13},{13,15},{2,0},{4,2},{6,4},{... | collective-permute-start | bytes 147464 | tf_op jit(solution)/shard_map/ppermute | solution.py:455
  4.0 0.1 pad_add_fusion.1.info_ref
  4.7 0.3 fusion
  5.0 0.1 pad_add_fusion.info_ref
  5.1 1.6 %shard_map.113 = (bf16[56,1536]{1,0:T(8,128)(2,1)S(1)}, f32[31,1536]{1,0:T(8,128)S(1)}, f32[5,1536]{1,0:T(8,128)S(1)}) custom-call(s32[2]{0:T(128)S(1)} %pad_add_fusion.1.info_ref, bf16[2,56,1536]{2,1,0:T(8,128)(2,1)} %hidden_hbm.1, f32[31,1536]{1,0:T(8,128)} %taps_hbm.1, f32[5,1536]{1,0:T(8,128)} %mod_hbm.1), custom_call_target="tpu_custom_call" | custom-call | tf_op jit(solution)/shard_map/pallas_call | solution.py:291
  6.7 0.0 collective-permute-done.1.near_ref
  6.7 3.7 %collective-permute-done.2.far_ref = bf16[16,1536]{1,0:T(8,128)(2,1)S(1)} collective-permute-done((bf16[16,1536]{1,0:T(8,128)(2,1)S(1)}, bf16[16,1536]{1,0:T(8,128)(2,1)S(1)}, u32[]{:S(2)}, u32[]{:S(2)}) %collective-permute-start.2) | collective-permute-done | bytes 49184 | tf_op jit(solution)/shard_map/ppermute | solution.py:455
  10.4 0.0 collective-permute-done.partner_ref
  10.4 4.3 %shard_map.114 = (f32[112,1536]{1,0:T(8,128)S(1)}, bf16[112,1536]{1,0:T(8,128)(2,1)S(1)}, bf16[1536,3072]{1,0:T(8,128)(2,1)S(1)}) custom-call(s32[3]{0:T(128)S(1)} %pad_add_fusion.info_ref, bf16[56,1536]{1,0:T(8,128)(2,1)S(1)} %get-tuple-element.18.own_ref, bf16[2,56,1536]{2,1,0:T(8,128)(2,1)S(1)} %collective-permute-done.partner_ref, ...), custom_call_target="tpu_custom_call" | custom-call | tf_op jit(solution)/shard_map/pallas_call | solution.py:291
  14.8 0.0 copy-start.1
  14.8 1.2 %shard_map.118 = (bf16[3,112,128]{2,1,0:T(8,128)(2,1)S(1)}, bf16[3,112,128]{2,1,0:T(8,128)(2,1)S(1)}) custom-call(s32[3]{0:T(128)S(1)} %pad_add_fusion.info_ref, bf16[112,1536]{1,0:T(8,128)(2,1)S(1)} %get-tuple-element.22.normed_ref, bf16[1536,3072]{1,0:T(8,128)(2,1)S(1)} %get-tuple-element.23.weight_ref, f32[112,128]{1,0:T(8,128)S(1)} %get-tuple-element.39.cos_ref, ...), custom_call_target="tpu_custom_call" | custom-call | tf_op jit(solution)/shard_map/pallas_call | solution.py:291
  16.0 6.1 %collective-permute-start.8 = (bf16[3,112,128]{2,1,0:T(8,128)(2,1)S(1)}, bf16[3,112,128]{2,1,0:T(8,128)(2,1)S(1)}, u32[]{:S(2)}, u32[]{:S(2)}) collective-permute-start(bf16[3,112,128]{2,1,0:T(8,128)(2,1)S(1)} %get-tuple-element.30), channel_id=1, source_target_pairs={{0,12},{1,13},{2,14},{3,15},{4,8},{5,9},{6,10},{7,11},{8,4},{9,5},... | collective-permute-start | bytes 258056 | tf_op jit(solution)/shard_map/ppermute | solution.py:321
  22.1 0.3 collective-permute-start.9
  22.4 1.2 %shard_map.117 = (bf16[3,112,128]{2,1,0:T(8,128)(2,1)S(1)}, bf16[3,112,128]{2,1,0:T(8,128)(2,1)S(1)}) custom-call(s32[3]{0:T(128)S(1)} %pad_add_fusion.info_ref, bf16[112,1536]{1,0:T(8,128)(2,1)S(1)} %get-tuple-element.22.normed_ref, bf16[1536,3072]{1,0:T(8,128)(2,1)S(1)} %get-tuple-element.23.weight_ref, f32[112,128]{1,0:T(8,128)S(1)} %get-tuple-element.39.cos_ref, ...), custom_call_target="tpu_custom_call" | custom-call | tf_op jit(solution)/shard_map/pallas_call | solution.py:291
  23.6 0.0 copy-done.1
  23.6 0.0 copy-start
  23.6 1.2 %shard_map.116 = (bf16[3,112,128]{2,1,0:T(8,128)(2,1)S(1)}, bf16[3,112,128]{2,1,0:T(8,128)(2,1)S(1)}) custom-call(s32[3]{0:T(128)S(1)} %pad_add_fusion.info_ref, bf16[112,1536]{1,0:T(8,128)(2,1)S(1)} %get-tuple-element.22.normed_ref, bf16[1536,3072]{1,0:T(8,128)(2,1)S(1)} %get-tuple-element.23.weight_ref, f32[112,128]{1,0:T(8,128)S(1)} %get-tuple-element.39.cos_ref, ...), custom_call_target="tpu_custom_call" | custom-call | tf_op jit(solution)/shard_map/pallas_call | solution.py:291
  24.8 0.0 copy-start.2
  24.8 1.2 %shard_map.115 = (bf16[3,112,128]{2,1,0:T(8,128)(2,1)S(1)}, bf16[3,112,128]{2,1,0:T(8,128)(2,1)S(1)}) custom-call(s32[3]{0:T(128)S(1)} %pad_add_fusion.info_ref, bf16[112,1536]{1,0:T(8,128)(2,1)S(1)} %get-tuple-element.22.normed_ref, bf16[1536,3072]{1,0:T(8,128)(2,1)S(1)} %get-tuple-element.23.weight_ref, f32[112,128]{1,0:T(8,128)S(1)} %get-tuple-element.39.cos_ref, ...), custom_call_target="tpu_custom_call" | custom-call | tf_op jit(solution)/shard_map/pallas_call | solution.py:291
  26.0 1.2 %collective-permute-start.6 = (bf16[3,112,128]{2,1,0:T(8,128)(2,1)S(1)}, bf16[3,112,128]{2,1,0:T(8,128)(2,1)S(1)}, u32[]{:S(2)}, u32[]{:S(2)}) collective-permute-start(bf16[3,112,128]{2,1,0:T(8,128)(2,1)S(1)} %get-tuple-element.28), channel_id=1, source_target_pairs={{0,8},{1,9},{2,10},{3,11},{4,12},{5,13},{6,14},{7,15},{8,0},{9,1},... | collective-permute-start | bytes 258056 | tf_op jit(solution)/shard_map/ppermute | solution.py:321
  27.2 2.4 %collective-permute-start.7 = (bf16[3,112,128]{2,1,0:T(8,128)(2,1)S(1)}, bf16[3,112,128]{2,1,0:T(8,128)(2,1)S(1)}, u32[]{:S(2)}, u32[]{:S(2)}) collective-permute-start(bf16[3,112,128]{2,1,0:T(8,128)(2,1)S(1)} %get-tuple-element.29), channel_id=1, source_target_pairs={{0,10},{1,11},{2,8},{3,9},{4,14},{5,15},{6,12},{7,13},{8,2},{9,3},... | collective-permute-start | bytes 258056 | tf_op jit(solution)/shard_map/ppermute | solution.py:321
  29.7 1.5 %collective-permute-start.4 = (bf16[3,112,128]{2,1,0:T(8,128)(2,1)S(1)}, bf16[3,112,128]{2,1,0:T(8,128)(2,1)S(1)}, u32[]{:S(2)}, u32[]{:S(2)}) collective-permute-start(bf16[3,112,128]{2,1,0:T(8,128)(2,1)S(1)} %get-tuple-element.26), channel_id=1, source_target_pairs={{0,4},{1,5},{2,6},{3,7},{4,0},{5,1},{6,2},{7,3},{8,12},{9,13},{10,... | collective-permute-start | bytes 258056 | tf_op jit(solution)/shard_map/ppermute | solution.py:321
  31.2 0.0 collective-permute-done.8.refs_6_
  31.2 0.7 %collective-permute-start.5 = (bf16[3,112,128]{2,1,0:T(8,128)(2,1)S(1)}, bf16[3,112,128]{2,1,0:T(8,128)(2,1)S(1)}, u32[]{:S(2)}, u32[]{:S(2)}) collective-permute-start(bf16[3,112,128]{2,1,0:T(8,128)(2,1)S(1)} %get-tuple-element.27), channel_id=1, source_target_pairs={{0,6},{1,7},{2,4},{3,5},{4,2},{5,3},{6,0},{7,1},{8,14},{9,15},{10,... | collective-permute-start | bytes 258056 | tf_op jit(solution)/shard_map/ppermute | solution.py:321
  31.9 0.0 collective-permute-done.9.refs_7_
  31.9 1.2 %collective-permute-start.3 = (bf16[3,112,128]{2,1,0:T(8,128)(2,1)S(1)}, bf16[3,112,128]{2,1,0:T(8,128)(2,1)S(1)}, u32[]{:S(2)}, u32[]{:S(2)}) collective-permute-start(bf16[3,112,128]{2,1,0:T(8,128)(2,1)S(1)} %get-tuple-element.25), channel_id=1, source_target_pairs={{0,2},{1,3},{2,0},{3,1},{4,6},{5,7},{6,4},{7,5},{8,10},{9,11},{10,... | collective-permute-start | bytes 258056 | tf_op jit(solution)/shard_map/ppermute | solution.py:321
  33.1 1.1 %collective-permute-done.6.refs_4_ = bf16[3,112,128]{2,1,0:T(8,128)(2,1)S(1)} collective-permute-done((bf16[3,112,128]{2,1,0:T(8,128)(2,1)S(1)}, bf16[3,112,128]{2,1,0:T(8,128)(2,1)S(1)}, u32[]{:S(2)}, u32[]{:S(2)}) %collective-permute-start.6) | collective-permute-done | bytes 86048 | tf_op jit(solution)/shard_map/ppermute | solution.py:321
  34.3 3.1 %collective-permute-done.7.refs_5_ = bf16[3,112,128]{2,1,0:T(8,128)(2,1)S(1)} collective-permute-done((bf16[3,112,128]{2,1,0:T(8,128)(2,1)S(1)}, bf16[3,112,128]{2,1,0:T(8,128)(2,1)S(1)}, u32[]{:S(2)}, u32[]{:S(2)}) %collective-permute-start.7) | collective-permute-done | bytes 86048 | tf_op jit(solution)/shard_map/ppermute | solution.py:321
  37.4 0.0 collective-permute-done.4.refs_2_
  37.4 1.4 %collective-permute-done.5.refs_3_ = bf16[3,112,128]{2,1,0:T(8,128)(2,1)S(1)} collective-permute-done((bf16[3,112,128]{2,1,0:T(8,128)(2,1)S(1)}, bf16[3,112,128]{2,1,0:T(8,128)(2,1)S(1)}, u32[]{:S(2)}, u32[]{:S(2)}) %collective-permute-start.5) | collective-permute-done | bytes 86048 | tf_op jit(solution)/shard_map/ppermute | solution.py:321
  38.7 0.3 collective-permute-done.3.refs_1_
  39.0 4.3 %shard_map.119 = bf16[8,112,128]{2,1,0:T(8,128)(2,1)} custom-call(s32[3]{0:T(128)S(1)} %pad_add_fusion.info_ref, bf16[3,112,128]{2,1,0:T(8,128)(2,1)S(1)} %get-tuple-element.24.refs_0_, bf16[3,112,128]{2,1,0:T(8,128)(2,1)S(1)} %collective-permute-done.3.refs_1_, bf16[3,112,128]{2,1,0:T(8,128)(2,1)S(1)} %collective-permute-done.4.refs_2_, ...), custom_call_target="tpu_custom_call" | custom-call | tf_op jit(solution)/shard_map/pallas_call | solution.py:291
  43.3 4.4 %all-to-all-start = ((bf16[8,112,128]{2,1,0:T(8,128)(2,1)}), bf16[8,112,128]{2,1,0:T(8,128)(2,1)S(1)}, u32[]{:S(2)}, u32[]{:S(2)}) async-start(bf16[8,112,128]{2,1,0:T(8,128)(2,1)} %shard_map.119), calls=%async_computation | async-start | bytes 458752 | tf_op jit(solution)/shard_map/all_to_all | solution.py:429
  47.8 8.0 %all-to-all-done.got_ref = bf16[8,112,128]{2,1,0:T(8,128)(2,1)S(1)} async-done(((bf16[8,112,128]{2,1,0:T(8,128)(2,1)}), bf16[8,112,128]{2,1,0:T(8,128)(2,1)S(1)}, u32[]{:S(2)}, u32[]{:S(2)}) %all-to-all-start) | async-done | bytes 229408 | tf_op jit(solution)/shard_map/all_to_all | solution.py:429
  55.8 0.0 copy-done
  55.8 3.1 %shard_map.120 = (f32[56,100]{1,0:T(8,128)S(1)}, f32[56,100]{1,0:T(8,128)S(1)}) custom-call(s32[3]{0:T(128)S(1)} %pad_add_fusion.info_ref, f32[112,1536]{1,0:T(8,128)} %copy-done.1, bf16[100,1536]{1,0:T(8,128)(2,1)} %bitcast.12, f32[5,1536]{1,0:T(8,128)S(1)} %get-tuple-element.20.mod_ref, bf16[1024,1536]{1,0:T(8,128)(2,1)S(1)} %copy-done, ...), custom_call_target="tpu_custom_call" | custom-call | tf_op jit(solution)/shard_map/pallas_call | solution.py:291
  59.0 0.1 collective-permute-start.10
  60.4 0.0 collective-permute-done.10
  60.4 0.0 copy-done.2
  60.4 0.7 %multiply_add_fusion = (f32[56,100]{1,0:T(8,128)}, f32[56,100]{1,0:T(8,128)}) fusion(f32[56,100]{1,0:T(8,128)S(1)} %copy-done.2, f32[]{:T(128)} %bitcast.7, f32[56,100]{1,0:T(8,128)S(1)} %collective-permute-done.10, f32[56,100]{1,0:T(8,128)S(1)} %get-tuple-element.32, f32[]{:T(128)} %bitcast.11, pred[]{:T(512)S(6)} %eq.7, pred[56]{0:T(512)(128)(4,1)S(1)} %add_compare_fusion), kind=kLoop, calls=%fused_computation.5 | loop fusion | flops 44800 | bytes 112065 | tf_op jit(solution)/shard_map/add | solution.py:513
  (3 shorter events, 0.0 us)
Async XLA Ops:
  0.6 9.8 %collective-permute-start = (bf16[2,56,1536]{2,1,0:T(8,128)(2,1)}, bf16[2,56,1536]{2,1,0:T(8,128)(2,1)S(1)}, u32[]{:S(2)}, u32[]{:S(2)}) collective-permute-start(bf16[2,56,1536]{2,1,0:T(8,128)(2,1)} %hidden_hbm.1), channel_id=1, source_target_pairs={{0,1},{1,0},{2,3},{3,2},{4,5},{5,4},{6,7},{7,6},{8,9},{9,8},{10,11... | collective-permute-start | bytes 1032200 | tf_op jit(solution)/shard_map/ppermute | solution.py:321
  2.0 4.7 %collective-permute-start.1 = (bf16[16,1536]{1,0:T(8,128)(2,1)S(1)}, bf16[16,1536]{1,0:T(8,128)(2,1)S(1)}, u32[]{:S(2)}, u32[]{:S(2)}) collective-permute-start(bf16[16,1536]{1,0:T(8,128)(2,1)S(1)} %get-tuple-element.37), channel_id=1, source_target_pairs={{1,2},{3,4},{5,6},{7,8},{9,10},{11,12},{13,14},{2,1},{4,3},{6,5},{... | collective-permute-start | bytes 147464 | tf_op jit(solution)/shard_map/ppermute | solution.py:451
  2.7 7.8 %collective-permute-start.2 = (bf16[16,1536]{1,0:T(8,128)(2,1)S(1)}, bf16[16,1536]{1,0:T(8,128)(2,1)S(1)}, u32[]{:S(2)}, u32[]{:S(2)}) collective-permute-start(bf16[16,1536]{1,0:T(8,128)(2,1)S(1)} %get-tuple-element.36), channel_id=1, source_target_pairs={{1,3},{3,5},{5,7},{7,9},{9,11},{11,13},{13,15},{2,0},{4,2},{6,4},{... | collective-permute-start | bytes 147464 | tf_op jit(solution)/shard_map/ppermute | solution.py:455
  14.8 8.8 %copy-start.1 = (f32[112,1536]{1,0:T(8,128)}, f32[112,1536]{1,0:T(8,128)S(1)}, u32[]{:S(2)}) copy-start(f32[112,1536]{1,0:T(8,128)S(1)} %get-tuple-element.21.residual_hbm) | copy-start | bytes 2064388
  16.0 15.2 %collective-permute-start.8 = (bf16[3,112,128]{2,1,0:T(8,128)(2,1)S(1)}, bf16[3,112,128]{2,1,0:T(8,128)(2,1)S(1)}, u32[]{:S(2)}, u32[]{:S(2)}) collective-permute-start(bf16[3,112,128]{2,1,0:T(8,128)(2,1)S(1)} %get-tuple-element.30), channel_id=1, source_target_pairs={{0,12},{1,13},{2,14},{3,15},{4,8},{5,9},{6,10},{7,11},{8,4},{9,5},... | collective-permute-start | bytes 258056 | tf_op jit(solution)/shard_map/ppermute | solution.py:321
  22.1 9.8 %collective-permute-start.9 = (bf16[3,112,128]{2,1,0:T(8,128)(2,1)S(1)}, bf16[3,112,128]{2,1,0:T(8,128)(2,1)S(1)}, u32[]{:S(2)}, u32[]{:S(2)}) collective-permute-start(bf16[3,112,128]{2,1,0:T(8,128)(2,1)S(1)} %get-tuple-element.31), channel_id=1, source_target_pairs={{0,14},{1,15},{2,12},{3,13},{4,10},{5,11},{6,8},{7,9},{8,6},{9,7},... | collective-permute-start | bytes 258056 | tf_op jit(solution)/shard_map/ppermute | solution.py:321
  23.6 32.2 %copy-start = (bf16[1024,1536]{1,0:T(8,128)(2,1)S(1)}, bf16[1024,1536]{1,0:T(8,128)(2,1)}, u32[]{:S(2)}) copy-start(bf16[1024,1536]{1,0:T(8,128)(2,1)} %w_out_ref.1) | copy-start | bytes 9437188
  24.8 35.6 %copy-start.2 = (f32[56,100]{1,0:T(8,128)S(1)}, f32[56,100]{1,0:T(8,128)}, u32[]{:S(2)}) copy-start(f32[56,100]{1,0:T(8,128)} %param.11) | copy-start | bytes 67204
  26.0 8.3 %collective-permute-start.6 = (bf16[3,112,128]{2,1,0:T(8,128)(2,1)S(1)}, bf16[3,112,128]{2,1,0:T(8,128)(2,1)S(1)}, u32[]{:S(2)}, u32[]{:S(2)}) collective-permute-start(bf16[3,112,128]{2,1,0:T(8,128)(2,1)S(1)} %get-tuple-element.28), channel_id=1, source_target_pairs={{0,8},{1,9},{2,10},{3,11},{4,12},{5,13},{6,14},{7,15},{8,0},{9,1},... | collective-permute-start | bytes 258056 | tf_op jit(solution)/shard_map/ppermute | solution.py:321
  27.2 10.1 %collective-permute-start.7 = (bf16[3,112,128]{2,1,0:T(8,128)(2,1)S(1)}, bf16[3,112,128]{2,1,0:T(8,128)(2,1)S(1)}, u32[]{:S(2)}, u32[]{:S(2)}) collective-permute-start(bf16[3,112,128]{2,1,0:T(8,128)(2,1)S(1)} %get-tuple-element.29), channel_id=1, source_target_pairs={{0,10},{1,11},{2,8},{3,9},{4,14},{5,15},{6,12},{7,13},{8,2},{9,3},... | collective-permute-start | bytes 258056 | tf_op jit(solution)/shard_map/ppermute | solution.py:321
  29.7 7.7 %collective-permute-start.4 = (bf16[3,112,128]{2,1,0:T(8,128)(2,1)S(1)}, bf16[3,112,128]{2,1,0:T(8,128)(2,1)S(1)}, u32[]{:S(2)}, u32[]{:S(2)}) collective-permute-start(bf16[3,112,128]{2,1,0:T(8,128)(2,1)S(1)} %get-tuple-element.26), channel_id=1, source_target_pairs={{0,4},{1,5},{2,6},{3,7},{4,0},{5,1},{6,2},{7,3},{8,12},{9,13},{10,... | collective-permute-start | bytes 258056 | tf_op jit(solution)/shard_map/ppermute | solution.py:321
  31.2 7.6 %collective-permute-start.5 = (bf16[3,112,128]{2,1,0:T(8,128)(2,1)S(1)}, bf16[3,112,128]{2,1,0:T(8,128)(2,1)S(1)}, u32[]{:S(2)}, u32[]{:S(2)}) collective-permute-start(bf16[3,112,128]{2,1,0:T(8,128)(2,1)S(1)} %get-tuple-element.27), channel_id=1, source_target_pairs={{0,6},{1,7},{2,4},{3,5},{4,2},{5,3},{6,0},{7,1},{8,14},{9,15},{10,... | collective-permute-start | bytes 258056 | tf_op jit(solution)/shard_map/ppermute | solution.py:321
  31.9 7.1 %collective-permute-start.3 = (bf16[3,112,128]{2,1,0:T(8,128)(2,1)S(1)}, bf16[3,112,128]{2,1,0:T(8,128)(2,1)S(1)}, u32[]{:S(2)}, u32[]{:S(2)}) collective-permute-start(bf16[3,112,128]{2,1,0:T(8,128)(2,1)S(1)} %get-tuple-element.25), channel_id=1, source_target_pairs={{0,2},{1,3},{2,0},{3,1},{4,6},{5,7},{6,4},{7,5},{8,10},{9,11},{10,... | collective-permute-start | bytes 258056 | tf_op jit(solution)/shard_map/ppermute | solution.py:321
  43.3 12.4 %all-to-all-start = ((bf16[8,112,128]{2,1,0:T(8,128)(2,1)}), bf16[8,112,128]{2,1,0:T(8,128)(2,1)S(1)}, u32[]{:S(2)}, u32[]{:S(2)}) async-start(bf16[8,112,128]{2,1,0:T(8,128)(2,1)} %shard_map.119), calls=%async_computation | async-start | bytes 458752 | tf_op jit(solution)/shard_map/all_to_all | solution.py:429
  59.0 1.5 %collective-permute-start.10 = (f32[56,100]{1,0:T(8,128)S(1)}, f32[56,100]{1,0:T(8,128)S(1)}, u32[]{:S(2)}, u32[]{:S(2)}) collective-permute-start(f32[56,100]{1,0:T(8,128)S(1)} %get-tuple-element.33), channel_id=1, source_target_pairs={{0,1},{1,0},{2,3},{3,2},{4,5},{5,4},{6,7},{7,6},{8,9},{9,8},{10,11... | collective-permute-start | bytes 67208 | tf_op jit(solution)/shard_map/ppermute | solution.py:321

commit v3 on v2

--- a/solution.py
+++ b/solution.py
@@ -127,7 +127,7 @@
         padded[near_at] = near_ref[:, lanes].astype(jnp.float32)
         padded[far_at] = far_ref[:, lanes].astype(jnp.float32)
         padded[own_at] = own_ref[:, lanes].astype(jnp.float32)
-        padded[partner_at] = partner_ref[core, :, lanes].astype(jnp.float32)
+        padded[partner_at] = partner_ref[:, lanes].astype(jnp.float32)
         own = padded[halo : halo + total_rows]
         padded[...] = padded[...] * live
         acc = jnp.zeros((total_rows, LANES), jnp.float32)
@@ -402,7 +402,8 @@
 
 
 def send_order(chips):
-    return list(range(chips // 2, chips, 2)) + list(range(2, chips // 2, 2)) + [0]
+    far = list(range(chips // 2, chips, 2))
+    return far[:1] + [0] + far[1:] + list(range(2, chips // 2, 2))
 
 
 def attend_chips(normed, w_qkv, tables, info, count):
@@ -443,10 +444,10 @@
     chip_rows = 2 * rows
     place = jnp.stack([core, chip])
 
-    partner = across(hidden, 1, count)
     edge = core * (rows - HALO)
     near = lax.dynamic_slice(hidden, (1 - core, edge, 0), (1, HALO, width))[0]
     far = lax.dynamic_slice(hidden, (core, edge, 0), (1, HALO, width))[0]
+    partner = lax.dynamic_slice(hidden, (1 - core, 0, 0), (1, rows, width))[0]
     steps = range(chips - 1)
     near = lax.ppermute(
         near, "seq",
@@ -456,6 +457,7 @@
         far, "seq",
         [(2 * m + 1, 2 * m + 3) for m in steps] + [(2 * m + 2, 2 * m) for m in steps],
     )
+    partner = across(partner, 1, count)
     own, taps, mods = call(
         stage_kernel,
         (

time: 61.5 us -> 62 us (level)
  waiting for transfers between devices: 17.6 us -> 14.3 us
  starting transfers between devices: 20.6 us -> 23.4 us
  local copies, waits for them, and re-layouts: 0.85 us -> 1.79 us
    ppermute x1, waiting for transfers between devices: 3.73 us -> 0.01 us  [per_device(): lax.ppermute(far, 'seq', [(2 * m + 1, 2 * m + 3) for m in steps] + [(2 *...]
    ppermute x9, starting transfers between devices: 14.2 us -> 17.6 us  [across(): return lax.ppermute(value, 'seq', [(i, i ^ apart) for i in range(count)])]
    squeeze x0 -> x1, local copies, waits for them, and re-layouts: none -> 0.94 us  [per_device(): partner = lax.dynamic_slice(hidden, (1 - core, 0, 0), (1, rows, width))[0]]
  transfers between devices with their start and end apart: 12 -> 12, of which waited for: 6 -> 5; matrix products, arithmetic and copies ran while one was open for 2% -> 2% of each run, Pallas kernels for 8% -> 8%
where the time goes in v3:
time: 62 us; the launch traced here: 61.6 us
  starting transfers between devices  23.4 us (38%)
  Pallas kernels  18.1 us (29%)
  waiting for transfers between devices  14.3 us (23%)
  between operations  2.85 us (5%)
  local copies, waits for them, and re-layouts  1.79 us (3%)
  other arithmetic  1.15 us (2%)
    pallas_call x8, Pallas kernels, call(): pl.pallas_call(kernel, out_shape=out_shape, in_specs=[smem_spec()] + spec...  18.1 us
    ppermute x9, starting transfers between devices, across(): return lax.ppermute(value, 'seq', [(i, i ^ apart) for i in range(count)])  17.6 us
    all_to_all x1, waiting for transfers between devices, attend_chips(): lax.all_to_all(attended, 'seq', split_axis=0, concat_axis=0, tiled=True,...  8 us
    ppermute x9, waiting for transfers between devices, across(): return lax.ppermute(value, 'seq', [(i, i ^ apart) for i in range(count)])  6.34 us
    all_to_all x1, starting transfers between devices, attend_chips(): lax.all_to_all(attended, 'seq', split_axis=0, concat_axis=0, tiled=True,...  3.83 us
    ppermute x1, starting transfers between devices, per_device(): lax.ppermute(far, 'seq', [(2 * m + 1, 2 * m + 3) for m in steps] + [(2 *...  1.29 us
  transfers between devices with their start and end apart: 12, of which 5 were waited for; matrix products, arithmetic and copies ran while one was open for 2% of the time, Pallas kernels for 8%

profile of v3, /device:TPU:0, one launch (start us, length us, event | category | flops | bytes accessed | tf_op | source)
XLA Modules:
  0.0 61.6 jit_solution(12301332204969584397)
XLA Ops:
  0.6 0.8 %dynamic-slice_bitcast_fusion.1 = (bf16[16,1536]{1,0:T(8,128)(2,1)S(1)}, bf16[16,1536]{1,0:T(8,128)(2,1)S(1)}) fusion(bf16[2,56,1536]{2,1,0:T(8,128)(2,1)} %hidden_hbm.1, s32[]{:T(128)S(6)} %select_n.57, s32[]{:T(128)S(6)} %select_n.56, s32[]{:T(128)S(6)} %select_n.55), kind=kLoop, calls=%fused_computation.4 | loop fusion | bytes 196620 | tf_op jit(solution)/shard_map/squeeze | solution.py:449
  1.5 0.7 %collective-permute-start.1 = (bf16[16,1536]{1,0:T(8,128)(2,1)S(1)}, bf16[16,1536]{1,0:T(8,128)(2,1)S(1)}, u32[]{:S(2)}, u32[]{:S(2)}) collective-permute-start(bf16[16,1536]{1,0:T(8,128)(2,1)S(1)} %get-tuple-element.37), channel_id=1, source_target_pairs={{1,2},{3,4},{5,6},{7,8},{9,10},{11,12},{13,14},{2,1},{4,3},{6,5},{... | collective-permute-start | bytes 147464 | tf_op jit(solution)/shard_map/ppermute | solution.py:452
  2.1 1.3 %collective-permute-start.2 = (bf16[16,1536]{1,0:T(8,128)(2,1)S(1)}, bf16[16,1536]{1,0:T(8,128)(2,1)S(1)}, u32[]{:S(2)}, u32[]{:S(2)}) collective-permute-start(bf16[16,1536]{1,0:T(8,128)(2,1)S(1)} %get-tuple-element.36), channel_id=1, source_target_pairs={{1,3},{3,5},{5,7},{7,9},{9,11},{11,13},{13,15},{2,0},{4,2},{6,4},{... | collective-permute-start | bytes 147464 | tf_op jit(solution)/shard_map/ppermute | solution.py:456
  3.4 0.9 %dynamic-slice_bitcast_fusion = bf16[56,1536]{1,0:T(8,128)(2,1)S(1)} fusion(bf16[2,56,1536]{2,1,0:T(8,128)(2,1)} %hidden_hbm.1, s32[]{:T(128)S(6)} %select_n.55), kind=kLoop, calls=%fused_computation | loop fusion | bytes 344068 | tf_op jit(solution)/shard_map/squeeze | solution.py:450
  4.4 6.3 %collective-permute-start = (bf16[56,1536]{1,0:T(8,128)(2,1)S(1)}, bf16[56,1536]{1,0:T(8,128)(2,1)S(1)}, u32[]{:S(2)}, u32[]{:S(2)}) collective-permute-start(bf16[56,1536]{1,0:T(8,128)(2,1)S(1)} %dynamic-slice_bitcast_fusion), channel_id=1, source_target_pairs={{0,1},{1,0},{2,3},{3,2},{4,5},{5,4},{6,7},{7,6},{8,9},{9,8},{10,11... | collective-permute-start | bytes 516104 | tf_op jit(solution)/shard_map/ppermute | solution.py:321
  11.3 0.3 fusion
  11.6 0.1 pad_add_fusion.1.info_ref
  11.7 0.1 pad_add_fusion.info_ref
  11.8 1.6 %shard_map.113 = (bf16[56,1536]{1,0:T(8,128)(2,1)S(1)}, f32[31,1536]{1,0:T(8,128)S(1)}, f32[5,1536]{1,0:T(8,128)S(1)}) custom-call(s32[2]{0:T(128)S(1)} %pad_add_fusion.1.info_ref, bf16[2,56,1536]{2,1,0:T(8,128)(2,1)} %hidden_hbm.1, f32[31,1536]{1,0:T(8,128)} %taps_hbm.1, f32[5,1536]{1,0:T(8,128)} %mod_hbm.1), custom_call_target="tpu_custom_call" | custom-call | tf_op jit(solution)/shard_map/pallas_call | solution.py:291
  13.4 0.0 collective-permute-done.1.near_ref
  13.4 0.0 collective-permute-done.2.far_ref
  13.4 0.0 collective-permute-done.partner_ref
  13.4 4.3 %shard_map.114 = (f32[112,1536]{1,0:T(8,128)S(1)}, bf16[112,1536]{1,0:T(8,128)(2,1)S(1)}, bf16[1536,3072]{1,0:T(8,128)(2,1)S(1)}) custom-call(s32[3]{0:T(128)S(1)} %pad_add_fusion.info_ref, bf16[56,1536]{1,0:T(8,128)(2,1)S(1)} %get-tuple-element.18.own_ref, bf16[56,1536]{1,0:T(8,128)(2,1)S(1)} %collective-permute-done.partner_ref, ...), custom_call_target="tpu_custom_call" | custom-call | tf_op jit(solution)/shard_map/pallas_call | solution.py:291
  17.7 0.0 copy-start.1
  17.7 1.2 %shard_map.118 = (bf16[3,112,128]{2,1,0:T(8,128)(2,1)S(1)}, bf16[3,112,128]{2,1,0:T(8,128)(2,1)S(1)}) custom-call(s32[3]{0:T(128)S(1)} %pad_add_fusion.info_ref, bf16[112,1536]{1,0:T(8,128)(2,1)S(1)} %get-tuple-element.22.normed_ref, bf16[1536,3072]{1,0:T(8,128)(2,1)S(1)} %get-tuple-element.23.weight_ref, f32[112,128]{1,0:T(8,128)S(1)} %get-tuple-element.39.cos_ref, ...), custom_call_target="tpu_custom_call" | custom-call | tf_op jit(solution)/shard_map/pallas_call | solution.py:291
  18.9 2.4 %collective-permute-start.8 = (bf16[3,112,128]{2,1,0:T(8,128)(2,1)S(1)}, bf16[3,112,128]{2,1,0:T(8,128)(2,1)S(1)}, u32[]{:S(2)}, u32[]{:S(2)}) collective-permute-start(bf16[3,112,128]{2,1,0:T(8,128)(2,1)S(1)} %get-tuple-element.30), channel_id=1, source_target_pairs={{0,12},{1,13},{2,14},{3,15},{4,8},{5,9},{6,10},{7,11},{8,4},{9,5},... | collective-permute-start | bytes 258056 | tf_op jit(solution)/shard_map/ppermute | solution.py:321
  21.3 2.4 %collective-permute-start.9 = (bf16[3,112,128]{2,1,0:T(8,128)(2,1)S(1)}, bf16[3,112,128]{2,1,0:T(8,128)(2,1)S(1)}, u32[]{:S(2)}, u32[]{:S(2)}) collective-permute-start(bf16[3,112,128]{2,1,0:T(8,128)(2,1)S(1)} %get-tuple-element.31), channel_id=1, source_target_pairs={{0,14},{1,15},{2,12},{3,13},{4,10},{5,11},{6,8},{7,9},{8,6},{9,7},... | collective-permute-start | bytes 258056 | tf_op jit(solution)/shard_map/ppermute | solution.py:321
  23.8 1.2 %shard_map.117 = (bf16[3,112,128]{2,1,0:T(8,128)(2,1)S(1)}, bf16[3,112,128]{2,1,0:T(8,128)(2,1)S(1)}) custom-call(s32[3]{0:T(128)S(1)} %pad_add_fusion.info_ref, bf16[112,1536]{1,0:T(8,128)(2,1)S(1)} %get-tuple-element.22.normed_ref, bf16[1536,3072]{1,0:T(8,128)(2,1)S(1)} %get-tuple-element.23.weight_ref, f32[112,128]{1,0:T(8,128)S(1)} %get-tuple-element.39.cos_ref, ...), custom_call_target="tpu_custom_call" | custom-call | tf_op jit(solution)/shard_map/pallas_call | solution.py:291
  24.9 0.0 copy-done.1
  25.0 0.0 copy-start
  25.0 1.2 %shard_map.116 = (bf16[3,112,128]{2,1,0:T(8,128)(2,1)S(1)}, bf16[3,112,128]{2,1,0:T(8,128)(2,1)S(1)}) custom-call(s32[3]{0:T(128)S(1)} %pad_add_fusion.info_ref, bf16[112,1536]{1,0:T(8,128)(2,1)S(1)} %get-tuple-element.22.normed_ref, bf16[1536,3072]{1,0:T(8,128)(2,1)S(1)} %get-tuple-element.23.weight_ref, f32[112,128]{1,0:T(8,128)S(1)} %get-tuple-element.39.cos_ref, ...), custom_call_target="tpu_custom_call" | custom-call | tf_op jit(solution)/shard_map/pallas_call | solution.py:291
  26.2 0.0 copy-start.2
  26.2 1.2 %shard_map.115 = (bf16[3,112,128]{2,1,0:T(8,128)(2,1)S(1)}, bf16[3,112,128]{2,1,0:T(8,128)(2,1)S(1)}) custom-call(s32[3]{0:T(128)S(1)} %pad_add_fusion.info_ref, bf16[112,1536]{1,0:T(8,128)(2,1)S(1)} %get-tuple-element.22.normed_ref, bf16[1536,3072]{1,0:T(8,128)(2,1)S(1)} %get-tuple-element.23.weight_ref, f32[112,128]{1,0:T(8,128)S(1)} %get-tuple-element.39.cos_ref, ...), custom_call_target="tpu_custom_call" | custom-call | tf_op jit(solution)/shard_map/pallas_call | solution.py:291
  27.3 0.9 %collective-permute-start.6 = (bf16[3,112,128]{2,1,0:T(8,128)(2,1)S(1)}, bf16[3,112,128]{2,1,0:T(8,128)(2,1)S(1)}, u32[]{:S(2)}, u32[]{:S(2)}) collective-permute-start(bf16[3,112,128]{2,1,0:T(8,128)(2,1)S(1)} %get-tuple-element.28), channel_id=1, source_target_pairs={{0,8},{1,9},{2,10},{3,11},{4,12},{5,13},{6,14},{7,15},{8,0},{9,1},... | collective-permute-start | bytes 258056 | tf_op jit(solution)/shard_map/ppermute | solution.py:321
  28.2 2.1 %collective-permute-start.7 = (bf16[3,112,128]{2,1,0:T(8,128)(2,1)S(1)}, bf16[3,112,128]{2,1,0:T(8,128)(2,1)S(1)}, u32[]{:S(2)}, u32[]{:S(2)}) collective-permute-start(bf16[3,112,128]{2,1,0:T(8,128)(2,1)S(1)} %get-tuple-element.29), channel_id=1, source_target_pairs={{0,10},{1,11},{2,8},{3,9},{4,14},{5,15},{6,12},{7,13},{8,2},{9,3},... | collective-permute-start | bytes 258056 | tf_op jit(solution)/shard_map/ppermute | solution.py:321
  30.3 0.1 collective-permute-start.4
  30.4 0.0 collective-permute-done.8.refs_6_
  30.4 2.9 %collective-permute-start.5 = (bf16[3,112,128]{2,1,0:T(8,128)(2,1)S(1)}, bf16[3,112,128]{2,1,0:T(8,128)(2,1)S(1)}, u32[]{:S(2)}, u32[]{:S(2)}) collective-permute-start(bf16[3,112,128]{2,1,0:T(8,128)(2,1)S(1)} %get-tuple-element.27), channel_id=1, source_target_pairs={{0,6},{1,7},{2,4},{3,5},{4,2},{5,3},{6,0},{7,1},{8,14},{9,15},{10,... | collective-permute-start | bytes 258056 | tf_op jit(solution)/shard_map/ppermute | solution.py:321
  33.3 0.0 collective-permute-done.9.refs_7_
  33.3 0.5 collective-permute-start.3
  33.8 2.1 %collective-permute-done.6.refs_4_ = bf16[3,112,128]{2,1,0:T(8,128)(2,1)S(1)} collective-permute-done((bf16[3,112,128]{2,1,0:T(8,128)(2,1)S(1)}, bf16[3,112,128]{2,1,0:T(8,128)(2,1)S(1)}, u32[]{:S(2)}, u32[]{:S(2)}) %collective-permute-start.6) | collective-permute-done | bytes 86048 | tf_op jit(solution)/shard_map/ppermute | solution.py:321
  35.9 2.4 %collective-permute-done.7.refs_5_ = bf16[3,112,128]{2,1,0:T(8,128)(2,1)S(1)} collective-permute-done((bf16[3,112,128]{2,1,0:T(8,128)(2,1)S(1)}, bf16[3,112,128]{2,1,0:T(8,128)(2,1)S(1)}, u32[]{:S(2)}, u32[]{:S(2)}) %collective-permute-start.7) | collective-permute-done | bytes 86048 | tf_op jit(solution)/shard_map/ppermute | solution.py:321
  38.3 0.0 collective-permute-done.4.refs_2_
  38.3 1.5 %collective-permute-done.5.refs_3_ = bf16[3,112,128]{2,1,0:T(8,128)(2,1)S(1)} collective-permute-done((bf16[3,112,128]{2,1,0:T(8,128)(2,1)S(1)}, bf16[3,112,128]{2,1,0:T(8,128)(2,1)S(1)}, u32[]{:S(2)}, u32[]{:S(2)}) %collective-permute-start.5) | collective-permute-done | bytes 86048 | tf_op jit(solution)/shard_map/ppermute | solution.py:321
  39.8 0.3 collective-permute-done.3.refs_1_
  40.1 4.3 %shard_map.119 = bf16[8,112,128]{2,1,0:T(8,128)(2,1)} custom-call(s32[3]{0:T(128)S(1)} %pad_add_fusion.info_ref, bf16[3,112,128]{2,1,0:T(8,128)(2,1)S(1)} %get-tuple-element.24.refs_0_, bf16[3,112,128]{2,1,0:T(8,128)(2,1)S(1)} %collective-permute-done.3.refs_1_, bf16[3,112,128]{2,1,0:T(8,128)(2,1)S(1)} %collective-permute-done.4.refs_2_, ...), custom_call_target="tpu_custom_call" | custom-call | tf_op jit(solution)/shard_map/pallas_call | solution.py:291
  44.4 3.8 %all-to-all-start = ((bf16[8,112,128]{2,1,0:T(8,128)(2,1)}), bf16[8,112,128]{2,1,0:T(8,128)(2,1)S(1)}, u32[]{:S(2)}, u32[]{:S(2)}) async-start(bf16[8,112,128]{2,1,0:T(8,128)(2,1)} %shard_map.119), calls=%async_computation | async-start | bytes 458752 | tf_op jit(solution)/shard_map/all_to_all | solution.py:430
  48.3 8.0 %all-to-all-done.got_ref = bf16[8,112,128]{2,1,0:T(8,128)(2,1)S(1)} async-done(((bf16[8,112,128]{2,1,0:T(8,128)(2,1)}), bf16[8,112,128]{2,1,0:T(8,128)(2,1)S(1)}, u32[]{:S(2)}, u32[]{:S(2)}) %all-to-all-start) | async-done | bytes 229408 | tf_op jit(solution)/shard_map/all_to_all | solution.py:430
  56.3 0.0 copy-done
  56.3 3.1 %shard_map.120 = (f32[56,100]{1,0:T(8,128)S(1)}, f32[56,100]{1,0:T(8,128)S(1)}) custom-call(s32[3]{0:T(128)S(1)} %pad_add_fusion.info_ref, f32[112,1536]{1,0:T(8,128)} %copy-done.1, bf16[100,1536]{1,0:T(8,128)(2,1)} %bitcast.14, f32[5,1536]{1,0:T(8,128)S(1)} %get-tuple-element.20.mod_ref, bf16[1024,1536]{1,0:T(8,128)(2,1)S(1)} %copy-done, ...), custom_call_target="tpu_custom_call" | custom-call | tf_op jit(solution)/shard_map/pallas_call | solution.py:291
  59.4 0.1 collective-permute-start.10
  60.9 0.0 collective-permute-done.10
  60.9 0.0 copy-done.2
  60.9 0.7 %multiply_add_fusion = (f32[56,100]{1,0:T(8,128)}, f32[56,100]{1,0:T(8,128)}) fusion(f32[56,100]{1,0:T(8,128)S(1)} %copy-done.2, f32[]{:T(128)} %bitcast.8, f32[56,100]{1,0:T(8,128)S(1)} %collective-permute-done.10, f32[56,100]{1,0:T(8,128)S(1)} %get-tuple-element.32, f32[]{:T(128)} %bitcast.13, pred[]{:T(512)S(6)} %eq.7, pred[56]{0:T(512)(128)(4,1)S(1)} %add_compare_fusion), kind=kLoop, calls=%fused_computation.6 | loop fusion | flops 44800 | bytes 112065 | tf_op jit(solution)/shard_map/add | solution.py:515
  (3 shorter events, 0.0 us)
Async XLA Ops:
  1.5 11.9 %collective-permute-start.1 = (bf16[16,1536]{1,0:T(8,128)(2,1)S(1)}, bf16[16,1536]{1,0:T(8,128)(2,1)S(1)}, u32[]{:S(2)}, u32[]{:S(2)}) collective-permute-start(bf16[16,1536]{1,0:T(8,128)(2,1)S(1)} %get-tuple-element.37), channel_id=1, source_target_pairs={{1,2},{3,4},{5,6},{7,8},{9,10},{11,12},{13,14},{2,1},{4,3},{6,5},{... | collective-permute-start | bytes 147464 | tf_op jit(solution)/shard_map/ppermute | solution.py:452
  2.1 11.2 %collective-permute-start.2 = (bf16[16,1536]{1,0:T(8,128)(2,1)S(1)}, bf16[16,1536]{1,0:T(8,128)(2,1)S(1)}, u32[]{:S(2)}, u32[]{:S(2)}) collective-permute-start(bf16[16,1536]{1,0:T(8,128)(2,1)S(1)} %get-tuple-element.36), channel_id=1, source_target_pairs={{1,3},{3,5},{5,7},{7,9},{9,11},{11,13},{13,15},{2,0},{4,2},{6,4},{... | collective-permute-start | bytes 147464 | tf_op jit(solution)/shard_map/ppermute | solution.py:456
  4.4 9.0 %collective-permute-start = (bf16[56,1536]{1,0:T(8,128)(2,1)S(1)}, bf16[56,1536]{1,0:T(8,128)(2,1)S(1)}, u32[]{:S(2)}, u32[]{:S(2)}) collective-permute-start(bf16[56,1536]{1,0:T(8,128)(2,1)S(1)} %dynamic-slice_bitcast_fusion), channel_id=1, source_target_pairs={{0,1},{1,0},{2,3},{3,2},{4,5},{5,4},{6,7},{7,6},{8,9},{9,8},{10,11... | collective-permute-start | bytes 516104 | tf_op jit(solution)/shard_map/ppermute | solution.py:321
  17.7 7.2 %copy-start.1 = (f32[112,1536]{1,0:T(8,128)}, f32[112,1536]{1,0:T(8,128)S(1)}, u32[]{:S(2)}) copy-start(f32[112,1536]{1,0:T(8,128)S(1)} %get-tuple-element.21.residual_hbm) | copy-start | bytes 2064388
  18.9 11.5 %collective-permute-start.8 = (bf16[3,112,128]{2,1,0:T(8,128)(2,1)S(1)}, bf16[3,112,128]{2,1,0:T(8,128)(2,1)S(1)}, u32[]{:S(2)}, u32[]{:S(2)}) collective-permute-start(bf16[3,112,128]{2,1,0:T(8,128)(2,1)S(1)} %get-tuple-element.30), channel_id=1, source_target_pairs={{0,12},{1,13},{2,14},{3,15},{4,8},{5,9},{6,10},{7,11},{8,4},{9,5},... | collective-permute-start | bytes 258056 | tf_op jit(solution)/shard_map/ppermute | solution.py:321
  21.3 11.9 %collective-permute-start.9 = (bf16[3,112,128]{2,1,0:T(8,128)(2,1)S(1)}, bf16[3,112,128]{2,1,0:T(8,128)(2,1)S(1)}, u32[]{:S(2)}, u32[]{:S(2)}) collective-permute-start(bf16[3,112,128]{2,1,0:T(8,128)(2,1)S(1)} %get-tuple-element.31), channel_id=1, source_target_pairs={{0,14},{1,15},{2,12},{3,13},{4,10},{5,11},{6,8},{7,9},{8,6},{9,7},... | collective-permute-start | bytes 258056 | tf_op jit(solution)/shard_map/ppermute | solution.py:321
  25.0 31.3 %copy-start = (bf16[1024,1536]{1,0:T(8,128)(2,1)S(1)}, bf16[1024,1536]{1,0:T(8,128)(2,1)}, u32[]{:S(2)}) copy-start(bf16[1024,1536]{1,0:T(8,128)(2,1)} %w_out_ref.1) | copy-start | bytes 9437188
  26.2 34.8 %copy-start.2 = (f32[56,100]{1,0:T(8,128)S(1)}, f32[56,100]{1,0:T(8,128)}, u32[]{:S(2)}) copy-start(f32[56,100]{1,0:T(8,128)} %param.11) | copy-start | bytes 67204
  27.3 8.6 %collective-permute-start.6 = (bf16[3,112,128]{2,1,0:T(8,128)(2,1)S(1)}, bf16[3,112,128]{2,1,0:T(8,128)(2,1)S(1)}, u32[]{:S(2)}, u32[]{:S(2)}) collective-permute-start(bf16[3,112,128]{2,1,0:T(8,128)(2,1)S(1)} %get-tuple-element.28), channel_id=1, source_target_pairs={{0,8},{1,9},{2,10},{3,11},{4,12},{5,13},{6,14},{7,15},{8,0},{9,1},... | collective-permute-start | bytes 258056 | tf_op jit(solution)/shard_map/ppermute | solution.py:321
  28.2 10.1 %collective-permute-start.7 = (bf16[3,112,128]{2,1,0:T(8,128)(2,1)S(1)}, bf16[3,112,128]{2,1,0:T(8,128)(2,1)S(1)}, u32[]{:S(2)}, u32[]{:S(2)}) collective-permute-start(bf16[3,112,128]{2,1,0:T(8,128)(2,1)S(1)} %get-tuple-element.29), channel_id=1, source_target_pairs={{0,10},{1,11},{2,8},{3,9},{4,14},{5,15},{6,12},{7,13},{8,2},{9,3},... | collective-permute-start | bytes 258056 | tf_op jit(solution)/shard_map/ppermute | solution.py:321
  30.3 8.0 %collective-permute-start.4 = (bf16[3,112,128]{2,1,0:T(8,128)(2,1)S(1)}, bf16[3,112,128]{2,1,0:T(8,128)(2,1)S(1)}, u32[]{:S(2)}, u32[]{:S(2)}) collective-permute-start(bf16[3,112,128]{2,1,0:T(8,128)(2,1)S(1)} %get-tuple-element.26), channel_id=1, source_target_pairs={{0,4},{1,5},{2,6},{3,7},{4,0},{5,1},{6,2},{7,3},{8,12},{9,13},{10,... | collective-permute-start | bytes 258056 | tf_op jit(solution)/shard_map/ppermute | solution.py:321
  30.4 9.4 %collective-permute-start.5 = (bf16[3,112,128]{2,1,0:T(8,128)(2,1)S(1)}, bf16[3,112,128]{2,1,0:T(8,128)(2,1)S(1)}, u32[]{:S(2)}, u32[]{:S(2)}) collective-permute-start(bf16[3,112,128]{2,1,0:T(8,128)(2,1)S(1)} %get-tuple-element.27), channel_id=1, source_target_pairs={{0,6},{1,7},{2,4},{3,5},{4,2},{5,3},{6,0},{7,1},{8,14},{9,15},{10,... | collective-permute-start | bytes 258056 | tf_op jit(solution)/shard_map/ppermute | solution.py:321
  33.3 6.8 %collective-permute-start.3 = (bf16[3,112,128]{2,1,0:T(8,128)(2,1)S(1)}, bf16[3,112,128]{2,1,0:T(8,128)(2,1)S(1)}, u32[]{:S(2)}, u32[]{:S(2)}) collective-permute-start(bf16[3,112,128]{2,1,0:T(8,128)(2,1)S(1)} %get-tuple-element.25), channel_id=1, source_target_pairs={{0,2},{1,3},{2,0},{3,1},{4,6},{5,7},{6,4},{7,5},{8,10},{9,11},{10,... | collective-permute-start | bytes 258056 | tf_op jit(solution)/shard_map/ppermute | solution.py:321
  44.4 11.8 %all-to-all-start = ((bf16[8,112,128]{2,1,0:T(8,128)(2,1)}), bf16[8,112,128]{2,1,0:T(8,128)(2,1)S(1)}, u32[]{:S(2)}, u32[]{:S(2)}) async-start(bf16[8,112,128]{2,1,0:T(8,128)(2,1)} %shard_map.119), calls=%async_computation | async-start | bytes 458752 | tf_op jit(solution)/shard_map/all_to_all | solution.py:430
  59.4 1.5 %collective-permute-start.10 = (f32[56,100]{1,0:T(8,128)S(1)}, f32[56,100]{1,0:T(8,128)S(1)}, u32[]{:S(2)}, u32[]{:S(2)}) collective-permute-start(f32[56,100]{1,0:T(8,128)S(1)} %get-tuple-element.33), channel_id=1, source_target_pairs={{0,1},{1,0},{2,3},{3,2},{4,5},{5,4},{6,7},{7,6},{8,9},{9,8},{10,11... | collective-permute-start | bytes 67208 | tf_op jit(solution)/shard_map/ppermute | solution.py:321

commit v4 on v3

--- a/solution.py
+++ b/solution.py
@@ -98,7 +98,7 @@
     residual_ref, normed_ref, weight_ref, padded, sems,
 ):
     rows, width = own_ref.shape
-    halo = near_ref.shape[0]
+    halo = near_ref.shape[1]
     total_rows = 2 * rows
     tiles = width // LANES
     parts = 8
@@ -115,7 +115,7 @@
     offset = info_ref[CHIP] * total_rows
     span = total_rows + 2 * halo
     frame = offset - halo + lax.broadcasted_iota(jnp.int32, (span, LANES), 0)
-    live = (frame < length).astype(jnp.float32)
+    live = ((frame >= 0) & (frame < length)).astype(jnp.float32)
     first = halo - KERNEL // 2
     own_at = pl.ds(pl.multiple_of(halo + core * rows, 8), rows)
     partner_at = pl.ds(pl.multiple_of(halo + (1 - core) * rows, 8), rows)
@@ -124,8 +124,8 @@
 
     def convolve(tile, total):
         lanes = tile_lanes(tile)
-        padded[near_at] = near_ref[:, lanes].astype(jnp.float32)
-        padded[far_at] = far_ref[:, lanes].astype(jnp.float32)
+        padded[near_at] = near_ref[core, :, lanes].astype(jnp.float32)
+        padded[far_at] = far_ref[core, :, lanes].astype(jnp.float32)
         padded[own_at] = own_ref[:, lanes].astype(jnp.float32)
         padded[partner_at] = partner_ref[:, lanes].astype(jnp.float32)
         own = padded[halo : halo + total_rows]
@@ -317,6 +317,17 @@
     return [list(range(core, count, 2)) for core in range(2)]
 
 
+def facing_pairs(clips, count):
+    pairs = []
+    for clip in range(clips):
+        base = clip * count
+        for at in range(1, count - 1, 2):
+            pairs += [(base + at, base + at + 1), (base + at + 1, base + at)]
+        if clip ^ 1 < clips:
+            pairs += [(base + end, (clip ^ 1) * count + end) for end in (0, count - 1)]
+    return pairs
+
+
 def across(value, apart, count):
     return lax.ppermute(value, "seq", [(i, i ^ apart) for i in range(count)])
 
@@ -436,27 +447,17 @@
 def per_device(
     hidden, latent, lengths, step_index, guidance, modulation, conv_kernel, w_qkv, w_out, w_mel
 ):
-    _, rows, width = hidden.shape
+    copies, rows, width = hidden.shape
     count = lax.axis_size("seq")
-    chips = count // 2
     index = lax.axis_index("seq").astype(jnp.int32)
     chip, core = index >> 1, index & 1
     chip_rows = 2 * rows
     place = jnp.stack([core, chip])
 
-    edge = core * (rows - HALO)
-    near = lax.dynamic_slice(hidden, (1 - core, edge, 0), (1, HALO, width))[0]
-    far = lax.dynamic_slice(hidden, (core, edge, 0), (1, HALO, width))[0]
+    edges = lax.dynamic_slice(hidden, (0, core * (rows - HALO), 0), (copies, HALO, width))
     partner = lax.dynamic_slice(hidden, (1 - core, 0, 0), (1, rows, width))[0]
-    steps = range(chips - 1)
-    near = lax.ppermute(
-        near, "seq",
-        [(2 * m + 1, 2 * m + 2) for m in steps] + [(2 * m + 2, 2 * m + 1) for m in steps],
-    )
-    far = lax.ppermute(
-        far, "seq",
-        [(2 * m + 1, 2 * m + 3) for m in steps] + [(2 * m + 2, 2 * m) for m in steps],
-    )
+    near = lax.ppermute(edges, ("clip", "seq"), facing_pairs(lax.axis_size("clip"), count))
+    far = across(near, 1, count)
     partner = across(partner, 1, count)
     own, taps, mods = call(
         stage_kernel,

time: 62 us -> 59.2 us (0.955)
  starting transfers between devices: 23.4 us -> 19.7 us
  waiting for transfers between devices: 14.3 us -> 15.2 us
    ppermute x9 -> x10, starting transfers between devices: 17.6 us -> 12 us  [across(): return lax.ppermute(value, 'seq', [(i, i ^ apart) for i in range(count)])]
    ppermute x2 -> x1, starting transfers between devices: 1.94 us -> 2.97 us  [per_device(): lax.ppermute(edges, ('clip', 'seq'), facing_pairs(lax.axis_size('clip'),...]
    all_to_all x1, starting transfers between devices: 3.83 us -> 4.79 us  [attend_chips(): lax.all_to_all(attended, 'seq', split_axis=0, concat_axis=0, tiled=True,...]
    dynamic_slice x0 -> x1, local copies, waits for them, and re-layouts: none -> 0.91 us  [per_device(): lax.dynamic_slice(hidden, (0, core * (rows - HALO), 0), (copies, HALO, wi...]
    ppermute x9 -> x10, waiting for transfers between devices: 6.34 us -> 7.22 us  [across(): return lax.ppermute(value, 'seq', [(i, i ^ apart) for i in range(count)])]
    squeeze x1 -> x0, local copies, waits for them, and re-layouts: 0.84 us -> none  [per_device(): far = lax.dynamic_slice(hidden, (core, edge, 0), (1, HALO, width))[0]]
  transfers between devices with their start and end apart: 12 -> 12, of which waited for: 5 -> 6; matrix products, arithmetic and copies ran while one was open for 2% -> 2% of each run, Pallas kernels for 8% -> 9%
where the time goes in v4:
time: 59.2 us; the launch traced here: 58.9 us
  starting transfers between devices  19.7 us (33%)
  Pallas kernels  18.1 us (31%)
  waiting for transfers between devices  15.2 us (26%)
  between operations  2.82 us (5%)
  local copies, waits for them, and re-layouts  1.85 us (3%)
  other arithmetic  1.15 us (2%)
    pallas_call x8, Pallas kernels, call(): pl.pallas_call(kernel, out_shape=out_shape, in_specs=[smem_spec()] + spec...  18.1 us
    ppermute x10, starting transfers between devices, across(): return lax.ppermute(value, 'seq', [(i, i ^ apart) for i in range(count)])  12 us
    all_to_all x1, waiting for transfers between devices, attend_chips(): lax.all_to_all(attended, 'seq', split_axis=0, concat_axis=0, tiled=True,...  8.01 us
    ppermute x10, waiting for transfers between devices, across(): return lax.ppermute(value, 'seq', [(i, i ^ apart) for i in range(count)])  7.22 us
    all_to_all x1, starting transfers between devices, attend_chips(): lax.all_to_all(attended, 'seq', split_axis=0, concat_axis=0, tiled=True,...  4.79 us
    ppermute x1, starting transfers between devices, per_device(): lax.ppermute(edges, ('clip', 'seq'), facing_pairs(lax.axis_size('clip'),...  2.97 us
  transfers between devices with their start and end apart: 12, of which 6 were waited for; matrix products, arithmetic and copies ran while one was open for 2% of the time, Pallas kernels for 9%

profile of v4, /device:TPU:0, one launch (start us, length us, event | category | flops | bytes accessed | tf_op | source)
XLA Modules:
  0.0 58.9 jit_solution(12773226603287248678)
XLA Ops:
  0.6 0.9 %constant_dynamic-slice_fusion = bf16[2,16,1536]{2,1,0:T(8,128)(2,1)S(1)} fusion(bf16[2,56,1536]{2,1,0:T(8,128)(2,1)} %hidden_hbm.1, s32[]{:T(128)S(6)} %select_n.51), kind=kLoop, calls=%fused_computation.16 | loop fusion | bytes 196612 | tf_op jit(solution)/shard_map/dynamic_slice | solution.py:457
  1.5 3.0 %collective-permute-start.1 = (bf16[2,16,1536]{2,1,0:T(8,128)(2,1)S(1)}, bf16[2,16,1536]{2,1,0:T(8,128)(2,1)S(1)}, u32[]{:S(2)}, u32[]{:S(2)}) collective-permute-start(bf16[2,16,1536]{2,1,0:T(8,128)(2,1)S(1)} %constant_dynamic-slice_fusion), channel_id=1, source_target_pairs={{1,2},{2,1},{3,4},{4,3},{5,6},{6,5},{7,8},{8,7},{9,10},{10,9},{11,... | collective-permute-start | bytes 294920 | tf_op jit(solution)/shard_map/ppermute | solution.py:459
  4.5 0.9 %dynamic-slice_bitcast_fusion = bf16[56,1536]{1,0:T(8,128)(2,1)S(1)} fusion(bf16[2,56,1536]{2,1,0:T(8,128)(2,1)} %hidden_hbm.1, s32[]{:T(128)S(6)} %select_n.50), kind=kLoop, calls=%fused_computation | loop fusion | bytes 344068 | tf_op jit(solution)/shard_map/squeeze | solution.py:458
  5.4 0.2 collective-permute-start
  6.3 0.3 fusion
  6.6 0.1 pad_add_fusion.1.info_ref
  6.7 1.6 %shard_map.113 = (bf16[56,1536]{1,0:T(8,128)(2,1)S(1)}, f32[31,1536]{1,0:T(8,128)S(1)}, f32[5,1536]{1,0:T(8,128)S(1)}) custom-call(s32[2]{0:T(128)S(1)} %pad_add_fusion.1.info_ref, bf16[2,56,1536]{2,1,0:T(8,128)(2,1)} %hidden_hbm.1, f32[31,1536]{1,0:T(8,128)} %taps_hbm.1, f32[5,1536]{1,0:T(8,128)} %mod_hbm.1), custom_call_target="tpu_custom_call" | custom-call | tf_op jit(solution)/shard_map/pallas_call | solution.py:291
  8.3 0.0 collective-permute-done.1.near_ref
  8.3 0.4 collective-permute-start.2
  8.7 0.1 pad_add_fusion.info_ref
  8.8 0.0 collective-permute-done.partner_ref
  8.8 0.9 %collective-permute-done.2.far_ref = bf16[2,16,1536]{2,1,0:T(8,128)(2,1)S(1)} collective-permute-done((bf16[2,16,1536]{2,1,0:T(8,128)(2,1)S(1)}, bf16[2,16,1536]{2,1,0:T(8,128)(2,1)S(1)}, u32[]{:S(2)}, u32[]{:S(2)}) %collective-permute-start.2) | collective-permute-done | bytes 98336 | tf_op jit(solution)/shard_map/ppermute | solution.py:332
  9.7 4.3 %shard_map.114 = (f32[112,1536]{1,0:T(8,128)S(1)}, bf16[112,1536]{1,0:T(8,128)(2,1)S(1)}, bf16[1536,3072]{1,0:T(8,128)(2,1)S(1)}) custom-call(s32[3]{0:T(128)S(1)} %pad_add_fusion.info_ref, bf16[56,1536]{1,0:T(8,128)(2,1)S(1)} %get-tuple-element.18.own_ref, bf16[56,1536]{1,0:T(8,128)(2,1)S(1)} %collective-permute-done.partner_ref, ...), custom_call_target="tpu_custom_call" | custom-call | tf_op jit(solution)/shard_map/pallas_call | solution.py:291
  14.0 0.0 copy-start.1
  14.0 1.2 %shard_map.118 = (bf16[3,112,128]{2,1,0:T(8,128)(2,1)S(1)}, bf16[3,112,128]{2,1,0:T(8,128)(2,1)S(1)}) custom-call(s32[3]{0:T(128)S(1)} %pad_add_fusion.info_ref, bf16[112,1536]{1,0:T(8,128)(2,1)S(1)} %get-tuple-element.22.normed_ref, bf16[1536,3072]{1,0:T(8,128)(2,1)S(1)} %get-tuple-element.23.weight_ref, f32[112,128]{1,0:T(8,128)S(1)} %get-tuple-element.37.cos_ref, ...), custom_call_target="tpu_custom_call" | custom-call | tf_op jit(solution)/shard_map/pallas_call | solution.py:291
  15.2 3.6 %collective-permute-start.8 = (bf16[3,112,128]{2,1,0:T(8,128)(2,1)S(1)}, bf16[3,112,128]{2,1,0:T(8,128)(2,1)S(1)}, u32[]{:S(2)}, u32[]{:S(2)}) collective-permute-start(bf16[3,112,128]{2,1,0:T(8,128)(2,1)S(1)} %get-tuple-element.30), channel_id=1, source_target_pairs={{0,12},{1,13},{2,14},{3,15},{4,8},{5,9},{6,10},{7,11},{8,4},{9,5},... | collective-permute-start | bytes 258056 | tf_op jit(solution)/shard_map/ppermute | solution.py:332
  18.8 1.2 %collective-permute-start.9 = (bf16[3,112,128]{2,1,0:T(8,128)(2,1)S(1)}, bf16[3,112,128]{2,1,0:T(8,128)(2,1)S(1)}, u32[]{:S(2)}, u32[]{:S(2)}) collective-permute-start(bf16[3,112,128]{2,1,0:T(8,128)(2,1)S(1)} %get-tuple-element.31), channel_id=1, source_target_pairs={{0,14},{1,15},{2,12},{3,13},{4,10},{5,11},{6,8},{7,9},{8,6},{9,7},... | collective-permute-start | bytes 258056 | tf_op jit(solution)/shard_map/ppermute | solution.py:332
  20.1 1.2 %shard_map.117 = (bf16[3,112,128]{2,1,0:T(8,128)(2,1)S(1)}, bf16[3,112,128]{2,1,0:T(8,128)(2,1)S(1)}) custom-call(s32[3]{0:T(128)S(1)} %pad_add_fusion.info_ref, bf16[112,1536]{1,0:T(8,128)(2,1)S(1)} %get-tuple-element.22.normed_ref, bf16[1536,3072]{1,0:T(8,128)(2,1)S(1)} %get-tuple-element.23.weight_ref, f32[112,128]{1,0:T(8,128)S(1)} %get-tuple-element.37.cos_ref, ...), custom_call_target="tpu_custom_call" | custom-call | tf_op jit(solution)/shard_map/pallas_call | solution.py:291
  21.2 0.0 copy-done.1
  21.2 0.0 copy-start
  21.2 1.2 %shard_map.116 = (bf16[3,112,128]{2,1,0:T(8,128)(2,1)S(1)}, bf16[3,112,128]{2,1,0:T(8,128)(2,1)S(1)}) custom-call(s32[3]{0:T(128)S(1)} %pad_add_fusion.info_ref, bf16[112,1536]{1,0:T(8,128)(2,1)S(1)} %get-tuple-element.22.normed_ref, bf16[1536,3072]{1,0:T(8,128)(2,1)S(1)} %get-tuple-element.23.weight_ref, f32[112,128]{1,0:T(8,128)S(1)} %get-tuple-element.37.cos_ref, ...), custom_call_target="tpu_custom_call" | custom-call | tf_op jit(solution)/shard_map/pallas_call | solution.py:291
  22.4 0.0 copy-start.2
  22.5 1.2 %shard_map.115 = (bf16[3,112,128]{2,1,0:T(8,128)(2,1)S(1)}, bf16[3,112,128]{2,1,0:T(8,128)(2,1)S(1)}) custom-call(s32[3]{0:T(128)S(1)} %pad_add_fusion.info_ref, bf16[112,1536]{1,0:T(8,128)(2,1)S(1)} %get-tuple-element.22.normed_ref, bf16[1536,3072]{1,0:T(8,128)(2,1)S(1)} %get-tuple-element.23.weight_ref, f32[112,128]{1,0:T(8,128)S(1)} %get-tuple-element.37.cos_ref, ...), custom_call_target="tpu_custom_call" | custom-call | tf_op jit(solution)/shard_map/pallas_call | solution.py:291
  23.6 0.9 %collective-permute-start.6 = (bf16[3,112,128]{2,1,0:T(8,128)(2,1)S(1)}, bf16[3,112,128]{2,1,0:T(8,128)(2,1)S(1)}, u32[]{:S(2)}, u32[]{:S(2)}) collective-permute-start(bf16[3,112,128]{2,1,0:T(8,128)(2,1)S(1)} %get-tuple-element.28), channel_id=1, source_target_pairs={{0,8},{1,9},{2,10},{3,11},{4,12},{5,13},{6,14},{7,15},{8,0},{9,1},... | collective-permute-start | bytes 258056 | tf_op jit(solution)/shard_map/ppermute | solution.py:332
  24.5 2.1 %collective-permute-start.7 = (bf16[3,112,128]{2,1,0:T(8,128)(2,1)S(1)}, bf16[3,112,128]{2,1,0:T(8,128)(2,1)S(1)}, u32[]{:S(2)}, u32[]{:S(2)}) collective-permute-start(bf16[3,112,128]{2,1,0:T(8,128)(2,1)S(1)} %get-tuple-element.29), channel_id=1, source_target_pairs={{0,10},{1,11},{2,8},{3,9},{4,14},{5,15},{6,12},{7,13},{8,2},{9,3},... | collective-permute-start | bytes 258056 | tf_op jit(solution)/shard_map/ppermute | solution.py:332
  26.6 1.3 %collective-permute-start.4 = (bf16[3,112,128]{2,1,0:T(8,128)(2,1)S(1)}, bf16[3,112,128]{2,1,0:T(8,128)(2,1)S(1)}, u32[]{:S(2)}, u32[]{:S(2)}) collective-permute-start(bf16[3,112,128]{2,1,0:T(8,128)(2,1)S(1)} %get-tuple-element.26), channel_id=1, source_target_pairs={{0,4},{1,5},{2,6},{3,7},{4,0},{5,1},{6,2},{7,3},{8,12},{9,13},{10,... | collective-permute-start | bytes 258056 | tf_op jit(solution)/shard_map/ppermute | solution.py:332
  27.9 0.0 collective-permute-done.8.refs_6_
  27.9 1.7 %collective-permute-start.5 = (bf16[3,112,128]{2,1,0:T(8,128)(2,1)S(1)}, bf16[3,112,128]{2,1,0:T(8,128)(2,1)S(1)}, u32[]{:S(2)}, u32[]{:S(2)}) collective-permute-start(bf16[3,112,128]{2,1,0:T(8,128)(2,1)S(1)} %get-tuple-element.27), channel_id=1, source_target_pairs={{0,6},{1,7},{2,4},{3,5},{4,2},{5,3},{6,0},{7,1},{8,14},{9,15},{10,... | collective-permute-start | bytes 258056 | tf_op jit(solution)/shard_map/ppermute | solution.py:332
  29.5 0.0 collective-permute-done.9.refs_7_
  29.5 0.5 collective-permute-start.3
  30.1 1.9 %collective-permute-done.6.refs_4_ = bf16[3,112,128]{2,1,0:T(8,128)(2,1)S(1)} collective-permute-done((bf16[3,112,128]{2,1,0:T(8,128)(2,1)S(1)}, bf16[3,112,128]{2,1,0:T(8,128)(2,1)S(1)}, u32[]{:S(2)}, u32[]{:S(2)}) %collective-permute-start.6) | collective-permute-done | bytes 86048 | tf_op jit(solution)/shard_map/ppermute | solution.py:332
  32.0 2.7 %collective-permute-done.7.refs_5_ = bf16[3,112,128]{2,1,0:T(8,128)(2,1)S(1)} collective-permute-done((bf16[3,112,128]{2,1,0:T(8,128)(2,1)S(1)}, bf16[3,112,128]{2,1,0:T(8,128)(2,1)S(1)}, u32[]{:S(2)}, u32[]{:S(2)}) %collective-permute-start.7) | collective-permute-done | bytes 86048 | tf_op jit(solution)/shard_map/ppermute | solution.py:332
  34.7 0.0 collective-permute-done.4.refs_2_
  34.7 1.3 %collective-permute-done.5.refs_3_ = bf16[3,112,128]{2,1,0:T(8,128)(2,1)S(1)} collective-permute-done((bf16[3,112,128]{2,1,0:T(8,128)(2,1)S(1)}, bf16[3,112,128]{2,1,0:T(8,128)(2,1)S(1)}, u32[]{:S(2)}, u32[]{:S(2)}) %collective-permute-start.5) | collective-permute-done | bytes 86048 | tf_op jit(solution)/shard_map/ppermute | solution.py:332
  36.0 0.4 collective-permute-done.3.refs_1_
  36.4 4.3 %shard_map.119 = bf16[8,112,128]{2,1,0:T(8,128)(2,1)} custom-call(s32[3]{0:T(128)S(1)} %pad_add_fusion.info_ref, bf16[3,112,128]{2,1,0:T(8,128)(2,1)S(1)} %get-tuple-element.24.refs_0_, bf16[3,112,128]{2,1,0:T(8,128)(2,1)S(1)} %collective-permute-done.3.refs_1_, bf16[3,112,128]{2,1,0:T(8,128)(2,1)S(1)} %collective-permute-done.4.refs_2_, ...), custom_call_target="tpu_custom_call" | custom-call | tf_op jit(solution)/shard_map/pallas_call | solution.py:291
  40.7 4.8 %all-to-all-start = ((bf16[8,112,128]{2,1,0:T(8,128)(2,1)}), bf16[8,112,128]{2,1,0:T(8,128)(2,1)S(1)}, u32[]{:S(2)}, u32[]{:S(2)}) async-start(bf16[8,112,128]{2,1,0:T(8,128)(2,1)} %shard_map.119), calls=%async_computation | async-start | bytes 458752 | tf_op jit(solution)/shard_map/all_to_all | solution.py:441
  45.5 8.0 %all-to-all-done.got_ref = bf16[8,112,128]{2,1,0:T(8,128)(2,1)S(1)} async-done(((bf16[8,112,128]{2,1,0:T(8,128)(2,1)}), bf16[8,112,128]{2,1,0:T(8,128)(2,1)S(1)}, u32[]{:S(2)}, u32[]{:S(2)}) %all-to-all-start) | async-done | bytes 229408 | tf_op jit(solution)/shard_map/all_to_all | solution.py:441
  53.5 0.0 copy-done
  53.5 3.1 %shard_map.120 = (f32[56,100]{1,0:T(8,128)S(1)}, f32[56,100]{1,0:T(8,128)S(1)}) custom-call(s32[3]{0:T(128)S(1)} %pad_add_fusion.info_ref, f32[112,1536]{1,0:T(8,128)} %copy-done.1, bf16[100,1536]{1,0:T(8,128)(2,1)} %bitcast.10, f32[5,1536]{1,0:T(8,128)S(1)} %get-tuple-element.20.mod_ref, bf16[1024,1536]{1,0:T(8,128)(2,1)S(1)} %copy-done, ...), custom_call_target="tpu_custom_call" | custom-call | tf_op jit(solution)/shard_map/pallas_call | solution.py:291
  56.7 0.1 collective-permute-start.10
  58.2 0.0 collective-permute-done.10
  58.2 0.0 copy-done.2
  58.2 0.7 %multiply_add_fusion = (f32[56,100]{1,0:T(8,128)}, f32[56,100]{1,0:T(8,128)}) fusion(f32[56,100]{1,0:T(8,128)S(1)} %copy-done.2, f32[]{:T(128)} %bitcast.6, f32[56,100]{1,0:T(8,128)S(1)} %collective-permute-done.10, f32[56,100]{1,0:T(8,128)S(1)} %get-tuple-element.32, f32[]{:T(128)} %bitcast.9, pred[]{:T(512)S(6)} %eq.7, pred[56]{0:T(512)(128)(4,1)S(1)} %add_compare_fusion), kind=kLoop, calls=%fused_computation.4 | loop fusion | flops 44800 | bytes 112065 | tf_op jit(solution)/shard_map/add | solution.py:516
  (3 shorter events, 0.0 us)
Async XLA Ops:
  1.5 6.7 %collective-permute-start.1 = (bf16[2,16,1536]{2,1,0:T(8,128)(2,1)S(1)}, bf16[2,16,1536]{2,1,0:T(8,128)(2,1)S(1)}, u32[]{:S(2)}, u32[]{:S(2)}) collective-permute-start(bf16[2,16,1536]{2,1,0:T(8,128)(2,1)S(1)} %constant_dynamic-slice_fusion), channel_id=1, source_target_pairs={{1,2},{2,1},{3,4},{4,3},{5,6},{6,5},{7,8},{8,7},{9,10},{10,9},{11,... | collective-permute-start | bytes 294920 | tf_op jit(solution)/shard_map/ppermute | solution.py:459
  5.4 3.4 %collective-permute-start = (bf16[56,1536]{1,0:T(8,128)(2,1)S(1)}, bf16[56,1536]{1,0:T(8,128)(2,1)S(1)}, u32[]{:S(2)}, u32[]{:S(2)}) collective-permute-start(bf16[56,1536]{1,0:T(8,128)(2,1)S(1)} %dynamic-slice_bitcast_fusion), channel_id=1, source_target_pairs={{0,1},{1,0},{2,3},{3,2},{4,5},{5,4},{6,7},{7,6},{8,9},{9,8},{10,11... | collective-permute-start | bytes 516104 | tf_op jit(solution)/shard_map/ppermute | solution.py:332
  8.3 1.4 %collective-permute-start.2 = (bf16[2,16,1536]{2,1,0:T(8,128)(2,1)S(1)}, bf16[2,16,1536]{2,1,0:T(8,128)(2,1)S(1)}, u32[]{:S(2)}, u32[]{:S(2)}) collective-permute-start(bf16[2,16,1536]{2,1,0:T(8,128)(2,1)S(1)} %collective-permute-done.1.near_ref), channel_id=1, source_target_pairs={{0,1},{1,0},{2,3},{3,2},{4,5},{5,4},{6,7},{7,6},{8,9},{9,8},{10,11... | collective-permute-start | bytes 294920 | tf_op jit(solution)/shard_map/ppermute | solution.py:332
  14.0 7.2 %copy-start.1 = (f32[112,1536]{1,0:T(8,128)}, f32[112,1536]{1,0:T(8,128)S(1)}, u32[]{:S(2)}) copy-start(f32[112,1536]{1,0:T(8,128)S(1)} %get-tuple-element.21.residual_hbm) | copy-start | bytes 2064388
  15.2 12.7 %collective-permute-start.8 = (bf16[3,112,128]{2,1,0:T(8,128)(2,1)S(1)}, bf16[3,112,128]{2,1,0:T(8,128)(2,1)S(1)}, u32[]{:S(2)}, u32[]{:S(2)}) collective-permute-start(bf16[3,112,128]{2,1,0:T(8,128)(2,1)S(1)} %get-tuple-element.30), channel_id=1, source_target_pairs={{0,12},{1,13},{2,14},{3,15},{4,8},{5,9},{6,10},{7,11},{8,4},{9,5},... | collective-permute-start | bytes 258056 | tf_op jit(solution)/shard_map/ppermute | solution.py:332
  18.8 10.7 %collective-permute-start.9 = (bf16[3,112,128]{2,1,0:T(8,128)(2,1)S(1)}, bf16[3,112,128]{2,1,0:T(8,128)(2,1)S(1)}, u32[]{:S(2)}, u32[]{:S(2)}) collective-permute-start(bf16[3,112,128]{2,1,0:T(8,128)(2,1)S(1)} %get-tuple-element.31), channel_id=1, source_target_pairs={{0,14},{1,15},{2,12},{3,13},{4,10},{5,11},{6,8},{7,9},{8,6},{9,7},... | collective-permute-start | bytes 258056 | tf_op jit(solution)/shard_map/ppermute | solution.py:332
  21.2 32.3 %copy-start = (bf16[1024,1536]{1,0:T(8,128)(2,1)S(1)}, bf16[1024,1536]{1,0:T(8,128)(2,1)}, u32[]{:S(2)}) copy-start(bf16[1024,1536]{1,0:T(8,128)(2,1)} %w_out_ref.1) | copy-start | bytes 9437188
  22.4 35.7 %copy-start.2 = (f32[56,100]{1,0:T(8,128)S(1)}, f32[56,100]{1,0:T(8,128)}, u32[]{:S(2)}) copy-start(f32[56,100]{1,0:T(8,128)} %param.11) | copy-start | bytes 67204
  23.6 8.4 %collective-permute-start.6 = (bf16[3,112,128]{2,1,0:T(8,128)(2,1)S(1)}, bf16[3,112,128]{2,1,0:T(8,128)(2,1)S(1)}, u32[]{:S(2)}, u32[]{:S(2)}) collective-permute-start(bf16[3,112,128]{2,1,0:T(8,128)(2,1)S(1)} %get-tuple-element.28), channel_id=1, source_target_pairs={{0,8},{1,9},{2,10},{3,11},{4,12},{5,13},{6,14},{7,15},{8,0},{9,1},... | collective-permute-start | bytes 258056 | tf_op jit(solution)/shard_map/ppermute | solution.py:332
  24.5 10.2 %collective-permute-start.7 = (bf16[3,112,128]{2,1,0:T(8,128)(2,1)S(1)}, bf16[3,112,128]{2,1,0:T(8,128)(2,1)S(1)}, u32[]{:S(2)}, u32[]{:S(2)}) collective-permute-start(bf16[3,112,128]{2,1,0:T(8,128)(2,1)S(1)} %get-tuple-element.29), channel_id=1, source_target_pairs={{0,10},{1,11},{2,8},{3,9},{4,14},{5,15},{6,12},{7,13},{8,2},{9,3},... | collective-permute-start | bytes 258056 | tf_op jit(solution)/shard_map/ppermute | solution.py:332
  26.6 8.1 %collective-permute-start.4 = (bf16[3,112,128]{2,1,0:T(8,128)(2,1)S(1)}, bf16[3,112,128]{2,1,0:T(8,128)(2,1)S(1)}, u32[]{:S(2)}, u32[]{:S(2)}) collective-permute-start(bf16[3,112,128]{2,1,0:T(8,128)(2,1)S(1)} %get-tuple-element.26), channel_id=1, source_target_pairs={{0,4},{1,5},{2,6},{3,7},{4,0},{5,1},{6,2},{7,3},{8,12},{9,13},{10,... | collective-permute-start | bytes 258056 | tf_op jit(solution)/shard_map/ppermute | solution.py:332
  27.9 8.1 %collective-permute-start.5 = (bf16[3,112,128]{2,1,0:T(8,128)(2,1)S(1)}, bf16[3,112,128]{2,1,0:T(8,128)(2,1)S(1)}, u32[]{:S(2)}, u32[]{:S(2)}) collective-permute-start(bf16[3,112,128]{2,1,0:T(8,128)(2,1)S(1)} %get-tuple-element.27), channel_id=1, source_target_pairs={{0,6},{1,7},{2,4},{3,5},{4,2},{5,3},{6,0},{7,1},{8,14},{9,15},{10,... | collective-permute-start | bytes 258056 | tf_op jit(solution)/shard_map/ppermute | solution.py:332
  29.5 6.9 %collective-permute-start.3 = (bf16[3,112,128]{2,1,0:T(8,128)(2,1)S(1)}, bf16[3,112,128]{2,1,0:T(8,128)(2,1)S(1)}, u32[]{:S(2)}, u32[]{:S(2)}) collective-permute-start(bf16[3,112,128]{2,1,0:T(8,128)(2,1)S(1)} %get-tuple-element.25), channel_id=1, source_target_pairs={{0,2},{1,3},{2,0},{3,1},{4,6},{5,7},{6,4},{7,5},{8,10},{9,11},{10,... | collective-permute-start | bytes 258056 | tf_op jit(solution)/shard_map/ppermute | solution.py:332
  40.7 12.8 %all-to-all-start = ((bf16[8,112,128]{2,1,0:T(8,128)(2,1)}), bf16[8,112,128]{2,1,0:T(8,128)(2,1)S(1)}, u32[]{:S(2)}, u32[]{:S(2)}) async-start(bf16[8,112,128]{2,1,0:T(8,128)(2,1)} %shard_map.119), calls=%async_computation | async-start | bytes 458752 | tf_op jit(solution)/shard_map/all_to_all | solution.py:441
  56.7 1.5 %collective-permute-start.10 = (f32[56,100]{1,0:T(8,128)S(1)}, f32[56,100]{1,0:T(8,128)S(1)}, u32[]{:S(2)}, u32[]{:S(2)}) collective-permute-start(f32[56,100]{1,0:T(8,128)S(1)} %get-tuple-element.33), channel_id=1, source_target_pairs={{0,1},{1,0},{2,3},{3,2},{4,5},{5,4},{6,7},{7,6},{8,9},{9,8},{10,11... | collective-permute-start | bytes 67208 | tf_op jit(solution)/shard_map/ppermute | solution.py:332
